TPU v7x, 32 devices: a whole 2x2x4 slice. The times are simulated.
32 devices in a mesh: dirs: 2 (over y), taps: 4 (over z), tm: 2 (over x), floors: 2 (over core).
Axes of the slice: x: 2, y: 2, z: 4, core: 2. Of those that a mesh axis runs over, the one named last changes fastest.
Arguments:
- pressures: bfloat16 [4096, 16384], P(('dirs', 'tm'), ('taps', 'floors')), parts along dimension 0, may hold values from -6 to 6
- tap_area: bfloat16 [16384], P(('taps', 'floors')), may hold values from 0.29882812 to 3
- tap_panel: int32 [16384], P(('taps', 'floors')), may hold values from 0 to 255
- tap_floor: int32 [16384], P(('taps', 'floors')), may hold values from 0 to 15
- panel_shape: bfloat16 [256, 512], replicated, may hold values from -0.046875 to 0.046875
- floor_shape: bfloat16 [16, 512], replicated, may hold values from -0.25 to 0.25
- mode_order: int32 [512], replicated, may hold values from 0 to 511, each once
- mode_decay: float32 [512], replicated, may hold values from 4.8828125e-05 to 0.08
- mode_freq: float32 [512], replicated, may hold values from 0.02 to 1.2
Outputs:
- modal_response: float32 [512, 4096], P(('taps', 'floors'), ('dirs', 'tm')), parts along dimension 1
- floor_motion: float32 [16, 4096], P(('taps', 'floors'), ('dirs', 'tm')), parts along dimension 1
- floor_load: float32 [16, 4096], P(('taps', 'floors'), ('dirs', 'tm')), parts along dimension 1
There are 2 independent parts, one for each index of `dirs`. A program takes and returns all parts, laid end to end along the dimension named above; an argument that names none is the same for every part. Nothing has to cross between parts.
All inputs are finite; a program needn't handle non-finite values.
Results may differ from a plain program's by a relative error of at most 0.0029.
Values sent between devices are 32-bit elements; how exact they have to be, the bound alone decides.
A program may use at most 64 MiB of HBM per device.

v0:
```python
import functools

import jax
import jax.numpy as jnp
from jax import lax
from jax.experimental import pallas as pl
from jax.experimental.pallas import tpu as pltpu
from jax.sharding import PartitionSpec as P

MESH = pl.DeviceIdType.MESH
LANES = 128
LAG = 2
NT = (((1,), (1,)), ((), ()))


def dot_nt(a, b):
    return lax.dot_general(a, b, NT, preferred_element_type=jnp.float32)


def dot_split(a, b):
    hi = b.astype(jnp.bfloat16)
    lo = (b - hi.astype(jnp.float32)).astype(jnp.bfloat16)
    return jnp.dot(a, hi, preferred_element_type=jnp.float32) + jnp.dot(
        a, lo, preferred_element_type=jnp.float32
    )


def kernel(
    cfg,
    p_hbm, area_h, panel_h, floor_h, shape_h, fshape_h, order_h, decay_h, freq_h,
    y_ref, fm_ref, fl_ref,
    area_ref, panel_ref, floor_ref, shape_ref, fshape_ref, order_ref, decay_ref, freq_ref, order_col,
    pv, w_ref, mine, send_p, recv_p, rin, lin, rout, lout, xs, fb, tabs, loc, loc_im, st_send, st_recv,
    fs, fr,
    in_sem, p_sem, pp_s, pp_r, r_s, r_r, l_s, l_r, x_s, x_r, t_s, t_r, f_s, f_r,
):
    nz, nc, ntm, splits = cfg
    owners = nz * nc
    z = lax.axis_index("taps")
    c = lax.axis_index("floors")
    x = lax.axis_index("tm")
    me = z * nc + c
    other = nc - 1 - c
    time_dev, taps = pv.shape
    panels, modes = shape_ref.shape
    floors = fshape_ref.shape[0]
    rows = panels + floors
    th = time_dev // nc
    tblocks = th // LANES
    crows = rows // splits
    nch = tblocks * splits
    md = modes // owners
    fd = floors // owners
    f32 = jnp.float32
    bf16 = jnp.bfloat16

    small = [
        pltpu.make_async_copy(src, dst, in_sem.at[i])
        for i, (src, dst) in enumerate(
            (
                (area_h, area_ref), (panel_h, panel_ref), (floor_h, floor_ref), (shape_h, shape_ref),
                (fshape_h, fshape_ref), (order_h, order_ref), (decay_h, decay_ref), (freq_h, freq_ref),
            )
        )
    ]
    for cp in small:
        cp.start()

    barrier = pltpu.get_barrier_semaphore()

    def greet(k, carry):
        j = lax.rem(me + k, owners)
        pl.semaphore_signal(
            barrier, inc=1, device_id={"taps": j // nc, "floors": lax.rem(j, nc)}, device_id_type=MESH
        )
        return carry

    lax.fori_loop(1, owners, greet, 0)
    for k in range(1, ntm):
        pl.semaphore_signal(
            barrier, inc=1, device_id={"tm": lax.rem(x + k, ntm)}, device_id_type=MESH
        )

    step_t = min(256, th)
    per_half = th // step_t
    loads = []
    for h in range(2):
        half = other if h == 0 else c
        for b in range(per_half):
            off = pl.multiple_of(half * th + b * step_t, step_t)
            cp = pltpu.make_async_copy(
                p_hbm.at[pl.ds(off, step_t)], pv.at[pl.ds(off, step_t)], p_sem.at[h * per_half + b]
            )
            cp.start()
            loads.append((cp, off))

    for cp in small[:3]:
        cp.wait()
    ids = lax.broadcasted_iota(jnp.int32, (panels, LANES), 0)
    fids = lax.broadcasted_iota(jnp.int32, (floors, LANES), 0)
    area = area_ref[...].astype(f32)
    for r in range(taps // LANES):
        cols = slice(r * LANES, (r + 1) * LANES)
        row = area[r : r + 1, :]
        w_ref[0:panels, cols] = jnp.where(panel_ref[:, cols] == ids, row, 0.0).astype(bf16)
        w_ref[panels:rows, cols] = jnp.where(floor_ref[:, cols] == fids, row, 0.0).astype(bf16)

    def sums(b, h, dst):
        cp, off = loads[h * per_half + b]
        cp.wait()
        q = dot_nt(w_ref[...], pv[pl.ds(off, step_t), :])
        for i in range(step_t // LANES):
            for s in range(splits):
                dst[(b * step_t // LANES + i) * splits + s] = q[
                    s * crows : (s + 1) * crows, i * LANES : (i + 1) * LANES
                ]

    def pair_copy(k):
        return pltpu.make_async_remote_copy(
            src_ref=send_p.at[k], dst_ref=recv_p.at[k], send_sem=pp_s.at[k], recv_sem=pp_r.at[k],
            device_id={"floors": other}, device_id_type=MESH,
        )

    per_step = step_t // LANES * splits

    @pl.when(z == 0)
    def _():
        rin[...] = jnp.zeros_like(rin)

    @pl.when(z == nz - 1)
    def _():
        lin[...] = jnp.zeros_like(lin)

    def line_copy(k, right):
        src, dst, ss, rs = (rout, rin, r_s, r_r) if right else (lout, lin, l_s, l_r)
        to = jnp.minimum(z + 1, nz - 1) if right else jnp.maximum(z - 1, 0)
        return pltpu.make_async_remote_copy(
            src_ref=src.at[k], dst_ref=dst.at[k], send_sem=ss.at[k], recv_sem=rs.at[k],
            device_id={"taps": to}, device_id_type=MESH,
        )

    def line_step(s, carry):
        for right in (True, False):
            hop = z if right else nz - 1 - z
            k = s - LAG * hop
            came, out = (rin, rout) if right else (lin, lout)

            @pl.when(jnp.logical_and(k >= 0, k < nch))
            def _():
                @pl.when(hop > 0)
                def _():
                    line_copy(k, right).wait_recv()

                @pl.when(hop < nz - 1)
                def _():
                    out[k] = mine[k] + came[k]
                    line_copy(k, right).start()

        return carry

    def merge(b):
        for k in range(b * per_step, (b + 1) * per_step):
            pair_copy(k).wait_recv()
            mine[k] = mine[k] + recv_p[k]

    for b in range(per_half):
        sums(b, 0, send_p)
        if b == 0:
            pl.semaphore_wait(barrier, owners - 1 + ntm - 1)
        for k in range(b * per_step, (b + 1) * per_step):
            pair_copy(k).start()
        if b > 0:
            merge(b - 1)
        if b == 1:
            lax.fori_loop(0, min(LAG, per_step), line_step, 0)
        sums(b, 1, mine)
    merge(per_half - 1)
    first = min(LAG, per_step) if per_half > 1 else 0
    early = min(LAG, nch)
    lax.fori_loop(first, early, line_step, 0)

    for cp in small[3:]:
        cp.wait()
    order_col[...] = jnp.transpose(jnp.broadcast_to(order_ref[...].astype(f32), (LANES, modes)))
    mode_ids = lax.broadcasted_iota(jnp.int32, (md, modes), 1).astype(f32)

    def pick(owner):
        return order_col[pl.ds(pl.multiple_of(owner * md, md), md), 0:1] == mode_ids

    def shapes(hot):
        return dot_nt(hot.astype(f32).astype(bf16), shape_ref[...]).astype(bf16)

    hot_me = pick(me)
    hot_other = pick(z * nc + other)
    g_both = jnp.concatenate([shapes(hot_other), shapes(hot_me)], axis=0)
    d = jnp.sum(jnp.where(hot_me, decay_ref[...], 0.0), axis=1, keepdims=True)
    w = jnp.sum(jnp.where(hot_me, freq_ref[...], 0.0), axis=1, keepdims=True)
    ls = dot_nt(fshape_ref[...], hot_me.astype(f32).astype(bf16)).astype(bf16)
    e2 = 2.0 * d
    poly = jnp.full_like(e2, 1.0 / 40320.0)
    for coef in (1.0 / 5040, 1.0 / 720, 1.0 / 120, 1.0 / 24, 1.0 / 6, 0.5, 1.0):
        poly = coef - e2 * poly
    gain = jnp.sqrt(e2 * poly)
    lane = lax.broadcasted_iota(jnp.int32, (md, LANES), 1)
    ahead = (lane + 1).astype(f32)
    mag = jnp.exp(-d * ahead)
    t_re = mag * jnp.cos(w * ahead)
    t_im = mag * jnp.sin(w * ahead)
    tabs[0] = t_re
    tabs[1] = t_im
    hops = []
    step = 1
    while step < LANES:
        i = 2 + 2 * len(hops)
        tabs[i] = jnp.where(lane >= step, t_re[:, step - 1 : step], 0.0)
        tabs[i + 1] = jnp.where(lane >= step, t_im[:, step - 1 : step], 0.0)
        hops.append(step)
        step *= 2

    floor_row = lax.broadcasted_iota(jnp.int32, (floors, LANES), 0)

    def load_row(q, row):
        return jnp.sum(jnp.where(floor_row == row, q, 0.0), axis=0, keepdims=True)

    def exchange(tb):
        return pltpu.make_async_remote_copy(
            src_ref=xs.at[tb], dst_ref=fb.at[c * tblocks + tb],
            send_sem=x_s.at[tb], recv_sem=x_r.at[tb],
            device_id={"floors": other}, device_id_type=MESH,
        )

    def forces(tb):
        q = jnp.concatenate(
            [mine[k] + rin[k] + lin[k] for k in range(tb * splits, (tb + 1) * splits)], axis=0
        )
        both = dot_split(g_both, q[:panels])
        blk = c * tblocks + tb
        pad = [jnp.zeros((xs.shape[1] - md - fd, LANES), f32)] if xs.shape[1] > md + fd else []
        theirs = [load_row(q[panels:], (z * nc + other) * fd + r) for r in range(fd)]
        ours = [load_row(q[panels:], me * fd + r) for r in range(fd)]
        xs[tb] = jnp.concatenate([both[:md]] + theirs + pad, axis=0)
        exchange(tb).start()
        fb[blk] = jnp.concatenate([both[md:]] + ours + pad, axis=0)

    def at_rest(blk):
        re = gain * fb[blk, 0:md, :]
        im = None
        for i, step in enumerate(hops):
            a, b = tabs[2 + 2 * i], tabs[3 + 2 * i]
            rr = pltpu.roll(re, step, 1)
            if im is None:
                re, im = re + a * rr, b * rr
            else:
                ri = pltpu.roll(im, step, 1)
                re, im = re + a * rr - b * ri, im + a * ri + b * rr
        loc[blk] = re
        loc_im[blk] = im

    done = early
    for tb in range(tblocks):
        upto = (tb + 1) * splits + LAG * (nz - 1)
        lax.fori_loop(done, upto, line_step, 0)
        done = upto
        forces(tb)
        at_rest(c * tblocks + tb)
        if tb > 0:
            exchange(tb - 1).wait_recv()
            at_rest(other * tblocks + tb - 1)
    exchange(tblocks - 1).wait_recv()
    at_rest(other * tblocks + tblocks - 1)
    nb = time_dev // LANES
    end_re = [loc[blk][:, LANES - 1 :] for blk in range(nb)]
    end_im = [loc_im[blk][:, LANES - 1 :] for blk in range(nb)]

    zb_re, zb_im = t_re[:, LANES - 1 :], t_im[:, LANES - 1 :]
    s_re, s_im = end_re[0], end_im[0]
    for blk in range(1, nb):
        s_re, s_im = (
            zb_re * s_re - zb_im * s_im + end_re[blk],
            zb_im * s_re + zb_re * s_im + end_im[blk],
        )

    def state_copy(to, src):
        return pltpu.make_async_remote_copy(
            src_ref=st_send, dst_ref=st_recv.at[src], send_sem=t_s.at[to], recv_sem=t_r.at[src],
            device_id={"tm": to}, device_id_type=MESH,
        )

    st_send[...] = jnp.where(lane == 0, s_re, s_im)
    in_re = jnp.zeros((md, 1), f32)
    in_im = jnp.zeros((md, 1), f32)
    if ntm > 1:
        for to in range(1, ntm):

            @pl.when(x < to)
            def _():
                state_copy(to, jnp.minimum(x, ntm - 2)).start()

        for src in range(ntm - 1):

            @pl.when(x > src)
            def _():
                state_copy(lax.rem(x + 1, ntm), src).wait_recv()

            @pl.when(x <= src)
            def _():
                st_recv[src] = jnp.zeros_like(st_send)

            got_re, got_im = st_recv[src][:, 0:1], st_recv[src][:, 1:2]
            if ntm == 2:
                in_re, in_im = got_re, got_im
                continue
            length = (jnp.maximum(x - 1 - src, 0) * time_dev).astype(f32)
            pm = jnp.exp(-d * length)
            pr, pi = pm * jnp.cos(w * length), pm * jnp.sin(w * length)
            in_re = in_re + pr * got_re - pi * got_im
            in_im = in_im + pi * got_re + pr * got_im

    t_re, t_im = tabs[0], tabs[1]
    for blk in range(nb):
        y = loc[blk] + t_re * in_re - t_im * in_im
        cols = slice(blk * LANES, (blk + 1) * LANES)
        y_ref[:, cols] = y
        in_re, in_im = (
            zb_re * in_re - zb_im * in_im + end_re[blk],
            zb_im * in_re + zb_re * in_im + end_im[blk],
        )
    part = dot_split(ls, y_ref[...])
    for j in range(owners):
        fs[j] = part[j * fd : (j + 1) * fd]

    def motion_copy(k):
        j = lax.rem(me + k, owners)
        return pltpu.make_async_remote_copy(
            src_ref=fs.at[j], dst_ref=fr.at[me], send_sem=f_s.at[k], recv_sem=f_r.at[k],
            device_id={"taps": j // nc, "floors": lax.rem(j, nc)}, device_id_type=MESH,
        )

    def motion_start(k, carry):
        motion_copy(k).start()
        return carry

    def motion_recv(k, total):
        motion_copy(k).wait_recv()
        return total + fr[lax.rem(me + owners - k, owners)]

    def motion_sent(k, carry):
        motion_copy(k).wait_send()
        return carry

    lax.fori_loop(1, owners, motion_start, 0)
    load_scale = (floors / (taps * owners)) ** 0.5
    for blk in range(nb):
        fl_ref[:, blk * LANES : (blk + 1) * LANES] = fb[blk, md : md + fd, :] * load_scale

    for k in range(nch):
        pair_copy(k).wait_send()

    def line_sent(k, carry):
        @pl.when(z < nz - 1)
        def _():
            line_copy(k, True).wait_send()

        @pl.when(z > 0)
        def _():
            line_copy(k, False).wait_send()

        return carry

    lax.fori_loop(0, nch, line_sent, 0)
    for tb in range(tblocks):
        exchange(tb).wait_send()
    for to in range(1, ntm):

        @pl.when(x < to)
        def _():
            state_copy(to, jnp.minimum(x, ntm - 2)).wait_send()

    fm_ref[...] = lax.fori_loop(1, owners, motion_recv, fs[me])
    lax.fori_loop(1, owners, motion_sent, 0)


def write_out(y, fm, fl, y_out, fm_out, fl_out, sem):
    copies = [
        pltpu.make_async_copy(src, dst, sem.at[i])
        for i, (src, dst) in enumerate(((y, y_out), (fm, fm_out), (fl, fl_out)))
    ]
    for cp in copies:
        cp.start()
    for cp in copies:
        cp.wait()


def on_device(
    pressures, tap_area, tap_panel, tap_floor, panel_shape, floor_shape, mode_order, mode_decay, mode_freq
):
    nz, nc, ntm = lax.axis_size("taps"), lax.axis_size("floors"), lax.axis_size("tm")
    owners = nz * nc
    time_dev, taps = pressures.shape
    panels, modes = panel_shape.shape
    floors = floor_shape.shape[0]
    rows = panels + floors
    splits = 2
    th = time_dev // nc
    md, fd = modes // owners, floors // owners
    nch = th // LANES * splits
    xrows = md + -(-fd // 8) * 8
    chunk = pltpu.VMEM((nch, rows // splits, LANES), jnp.float32)
    vmem = pl.BlockSpec(memory_space=pltpu.VMEM)
    dma = pltpu.SemaphoreType.DMA
    f32 = jnp.float32
    out = pl.pallas_call(
        functools.partial(kernel, (nz, nc, ntm, splits)),
        out_shape=(
            jax.ShapeDtypeStruct((md, time_dev), f32),
            jax.ShapeDtypeStruct((fd, time_dev), f32),
            jax.ShapeDtypeStruct((fd, time_dev), f32),
        ),
        in_specs=[pl.BlockSpec(memory_space=pltpu.HBM)] * 9,
        out_specs=(vmem,) * 3,
        scratch_shapes=[
            pltpu.VMEM((taps // LANES, LANES), jnp.bfloat16),
            pltpu.VMEM((1, taps), jnp.int32),
            pltpu.VMEM((1, taps), jnp.int32),
            pltpu.VMEM(panel_shape.shape, jnp.bfloat16),
            pltpu.VMEM(floor_shape.shape, jnp.bfloat16),
            pltpu.VMEM((1, modes), jnp.int32),
            pltpu.VMEM((1, modes), f32),
            pltpu.VMEM((1, modes), f32),
            pltpu.VMEM((modes, LANES), f32),
            pltpu.VMEM((time_dev, taps), jnp.bfloat16),
            pltpu.VMEM((rows, taps), jnp.bfloat16),
            chunk, chunk, chunk, chunk, chunk, chunk, chunk,
            pltpu.VMEM((th // LANES, xrows, LANES), f32),
            pltpu.VMEM((time_dev // LANES, xrows, LANES), f32),
            pltpu.VMEM((16, md, LANES), f32),
            pltpu.VMEM((time_dev // LANES, md, LANES), f32),
            pltpu.VMEM((time_dev // LANES, md, LANES), f32),
            pltpu.VMEM((md, LANES), f32),
            pltpu.VMEM((max(ntm - 1, 1), md, LANES), f32),
            pltpu.VMEM((owners, fd, time_dev), f32),
            pltpu.VMEM((owners, fd, time_dev), f32),
            dma((8,)),
            dma((2 * (th // min(256, th)),)),
            dma((nch,)), dma((nch,)), dma((nch,)), dma((nch,)), dma((nch,)), dma((nch,)),
            dma((th // LANES,)), dma((th // LANES,)),
            dma((ntm,)), dma((ntm,)),
            dma((owners,)), dma((owners,)),
        ],
        compiler_params=pltpu.CompilerParams(
            collective_id=0, has_side_effects=True, vmem_limit_bytes=67043328
        ),
    )(
        pressures,
        tap_area.reshape(taps // LANES, LANES),
        tap_panel.reshape(1, taps),
        tap_floor.reshape(1, taps),
        panel_shape,
        floor_shape,
        mode_order.reshape(1, modes),
        mode_decay.reshape(1, modes),
        mode_freq.reshape(1, modes),
    )
    return pl.pallas_call(
        write_out,
        out_shape=tuple(jax.ShapeDtypeStruct(o.shape, o.dtype) for o in out),
        in_specs=[vmem] * 3,
        out_specs=(pl.BlockSpec(memory_space=pltpu.HBM),) * 3,
        scratch_shapes=[dma((3,))],
        compiler_params=pltpu.CompilerParams(vmem_limit_bytes=67043328),
    )(*out)


def solution(mesh):
    own = P(("taps", "floors"))
    out_spec = P(("taps", "floors"), ("dirs", "tm"))
    return jax.shard_map(
        on_device,
        mesh=mesh,
        in_specs=(P(("dirs", "tm"), ("taps", "floors")), own, own, own, P(), P(), P(), P(), P()),
        out_specs=(out_spec, out_spec, out_spec),
        check_vma=False,
    )
```

profile of v0, /device:TPU:3, one launch (start us, length us, event | category | flops | bytes accessed | tf_op | source)
XLA Modules:
  0.0 39.1 jit_solution(15028898000378080421)
XLA Ops:
  0.6 36.7 %shard_map.112 = (f32[64,1024]{1,0:T(8,128)}, f32[2,1024]{1,0:T(2,128)}, f32[2,1024]{1,0:T(2,128)}) custom-call(bf16[1024,2048]{1,0:T(8,128)(2,1)} %p_hbm.1, bf16[16,128]{1,0:T(8,128)(2,1)} %bitcast.8, s32[1,2048]{1,0:T(1,128)} %bitcast.6, s32[1,2048]{1,0:T(1,128)} %bitcast.7, bf16[256,512]{1,0:T(8,128)(2,1)} %shape_h.1, bf16[16,512]{1,0:T(8,128)(2,1)} %fshape_h.1, ...), custom_call_target="tpu_custom_call" | custom-call | tf_op jit(solution)/shard_map/pallas_call | solution.py:412
  37.4 1.7 %shard_map.113 = (f32[64,1024]{1,0:T(8,128)}, f32[2,1024]{1,0:T(2,128)}, f32[2,1024]{1,0:T(2,128)}) custom-call(f32[64,1024]{1,0:T(8,128)} %get-tuple-element.6.y, f32[2,1024]{1,0:T(2,128)} %get-tuple-element.7.fm, f32[2,1024]{1,0:T(2,128)} %get-tuple-element.8.fl), custom_call_target="tpu_custom_call" | custom-call | tf_op jit(solution)/shard_map/pallas_call | solution.py:464
where the time goes:
time: 39.3 us; the launch traced here: 39.1 us
  Pallas kernels  38.4 us (98%)
  between operations  0.64 us (2%)
    pallas_call x1, Pallas kernels, on_device(): pl.pallas_call(functools.partial(kernel, (nz, nc, ntm, splits)), out_shap...  36.7 us
    pallas_call x1, Pallas kernels, on_device(): pl.pallas_call(write_out, out_shape=tuple((jax.ShapeDtypeStruct(o.shape,...  1.7 us

commit v1 on v0

--- a/solution.py
+++ b/solution.py
@@ -10,6 +10,7 @@
 MESH = pl.DeviceIdType.MESH
 LANES = 128
 LAG = 2
+VMEM_LIMIT = 32 * 1024 * 1024
 NT = (((1,), (1,)), ((), ()))
 
 
@@ -412,9 +413,9 @@
     out = pl.pallas_call(
         functools.partial(kernel, (nz, nc, ntm, splits)),
         out_shape=(
-            jax.ShapeDtypeStruct((md, time_dev), f32),
-            jax.ShapeDtypeStruct((fd, time_dev), f32),
-            jax.ShapeDtypeStruct((fd, time_dev), f32),
+            pltpu.VMEM((md, time_dev), f32),
+            pltpu.VMEM((fd, time_dev), f32),
+            pltpu.VMEM((fd, time_dev), f32),
         ),
         in_specs=[pl.BlockSpec(memory_space=pltpu.HBM)] * 9,
         out_specs=(vmem,) * 3,
@@ -448,18 +449,23 @@
             dma((owners,)), dma((owners,)),
         ],
         compiler_params=pltpu.CompilerParams(
-            collective_id=0, has_side_effects=True, vmem_limit_bytes=67043328
+            collective_id=0, has_side_effects=True, vmem_limit_bytes=VMEM_LIMIT
         ),
     )(
-        pressures,
-        tap_area.reshape(taps // LANES, LANES),
-        tap_panel.reshape(1, taps),
-        tap_floor.reshape(1, taps),
-        panel_shape,
-        floor_shape,
-        mode_order.reshape(1, modes),
-        mode_decay.reshape(1, modes),
-        mode_freq.reshape(1, modes),
+        *(
+            pltpu.with_memory_space_constraint(a, pltpu.HBM)
+            for a in (
+                pressures,
+                tap_area.reshape(taps // LANES, LANES),
+                tap_panel.reshape(1, taps),
+                tap_floor.reshape(1, taps),
+                panel_shape,
+                floor_shape,
+                mode_order.reshape(1, modes),
+                mode_decay.reshape(1, modes),
+                mode_freq.reshape(1, modes),
+            )
+        )
     )
     return pl.pallas_call(
         write_out,
@@ -467,7 +473,7 @@
         in_specs=[vmem] * 3,
         out_specs=(pl.BlockSpec(memory_space=pltpu.HBM),) * 3,
         scratch_shapes=[dma((3,))],
-        compiler_params=pltpu.CompilerParams(vmem_limit_bytes=67043328),
+        compiler_params=pltpu.CompilerParams(vmem_limit_bytes=VMEM_LIMIT),
     )(*out)
 
 

time: 39.3 us -> 37.6 us (0.957)
  the two profiles are of different devices: /device:TPU:3 before, /device:TPU:7 now
where the time goes in v1:
time: 37.6 us; the launch traced here: 37.4 us
  Pallas kernels  36.8 us (98%)
  between operations  0.64 us (2%)
    pallas_call x1, Pallas kernels, on_device(): pl.pallas_call(functools.partial(kernel, (nz, nc, ntm, splits)), out_shap...  36 us

profile of v1, /device:TPU:7, one launch (start us, length us, event | category | flops | bytes accessed | tf_op | source)
XLA Modules:
  0.0 37.4 jit_solution(9907818983567918670)
XLA Ops:
  0.6 36.0 %shard_map.112 = (f32[64,1024]{1,0:T(8,128)S(1)}, f32[2,1024]{1,0:T(2,128)S(1)}, f32[2,1024]{1,0:T(2,128)S(1)}) custom-call(bf16[1024,2048]{1,0:T(8,128)(2,1)} %p_hbm.1, bf16[16,128]{1,0:T(8,128)(2,1)} %bitcast.8, s32[1,2048]{1,0:T(1,128)} %bitcast.6, s32[1,2048]{1,0:T(1,128)} %bitcast.7, bf16[256,512]{1,0:T(8,128)(2,1)} %shape_h.1, ...), custom_call_target="tpu_custom_call" | custom-call | tf_op jit(solution)/shard_map/pallas_call | solution.py:413
  36.7 0.7 %shard_map.113 = (f32[64,1024]{1,0:T(8,128)}, f32[2,1024]{1,0:T(2,128)}, f32[2,1024]{1,0:T(2,128)}) custom-call(f32[64,1024]{1,0:T(8,128)S(1)} %get-tuple-element.6.y, f32[2,1024]{1,0:T(2,128)S(1)} %get-tuple-element.7.fm, f32[2,1024]{1,0:T(2,128)S(1)} %get-tuple-element.8.fl), custom_call_target="tpu_custom_call" | custom-call | tf_op jit(solution)/shard_map/pallas_call | solution.py:470

commit v2 on v1

--- a/solution.py
+++ b/solution.py
@@ -381,6 +381,389 @@
     lax.fori_loop(1, owners, motion_sent, 0)
 
 
+def two_stage(
+    cfg,
+    p_hbm, area_h, panel_h, floor_h, shape_h, fshape_h, order_h, decay_h, freq_h,
+    y_ref, fm_ref, fl_ref,
+    area_ref, panel_ref, floor_ref, shape_ref, fshape_ref, order_ref, decay_ref, freq_ref, order_col,
+    pv, w_ref, g_ref, send_p, recv_p, mine, up, sx, fx, si, fi, sp, fb, tabs, loc, loc_im, st_send, st_recv,
+    fls, flr, fs, fr,
+    in_sem, p_sem, pp_s, pp_r, u_s, u_r, x_s, x_r, i_s, i_r, e_s, e_r, fl_s, fl_r, t_s, t_r, f_s, f_r, known,
+):
+    nz, nc, ntm, pieces = cfg
+    owners = nz * nc
+    z = lax.axis_index("taps")
+    c = lax.axis_index("floors")
+    x = lax.axis_index("tm")
+    me = z * nc + c
+    other = nc - 1 - c
+    side = z // 2
+    mate = z + 1 - 2 * lax.rem(z, 2)
+    far = nz - 1 - z
+    inner = jnp.logical_or(z == 1, z == 2)
+    time_dev, taps = pv.shape
+    panels, modes = shape_ref.shape
+    floors = fshape_ref.shape[0]
+    rows = panels + floors
+    th = time_dev // nc
+    tblocks = th // LANES
+    md = modes // owners
+    fd = floors // owners
+    f32 = jnp.float32
+    bf16 = jnp.bfloat16
+
+    small = [
+        pltpu.make_async_copy(src, dst, in_sem.at[i])
+        for i, (src, dst) in enumerate(
+            (
+                (area_h, area_ref), (panel_h, panel_ref), (floor_h, floor_ref), (shape_h, shape_ref),
+                (fshape_h, fshape_ref), (order_h, order_ref), (decay_h, decay_ref), (freq_h, freq_ref),
+            )
+        )
+    ]
+    for cp in small[:3]:
+        cp.start()
+    loads = []
+    for i, (b, n) in enumerate(pieces):
+        for h, half in enumerate((other, c)):
+            off = pl.multiple_of(half * th + b * LANES, LANES)
+            cp = pltpu.make_async_copy(
+                p_hbm.at[pl.ds(off, n * LANES)], pv.at[pl.ds(off, n * LANES)], p_sem.at[2 * i + h]
+            )
+            cp.start()
+            loads.append((cp, off))
+    for cp in small[3:]:
+        cp.start()
+
+    barrier = pltpu.get_barrier_semaphore()
+
+    def greet(**to):
+        pl.semaphore_signal(barrier, inc=1, device_id=to, device_id_type=MESH)
+
+    greet(floors=other)
+    greet(taps=mate)
+    for k in range(1, ntm):
+        greet(tm=lax.rem(x + k, ntm))
+
+    @pl.when(inner)
+    def _():
+        greet(taps=far)
+
+    for cp in small[:3]:
+        cp.wait()
+    ids = lax.broadcasted_iota(jnp.int32, (panels, LANES), 0)
+    fids = lax.broadcasted_iota(jnp.int32, (floors, LANES), 0)
+    area = area_ref[...].astype(f32)
+    for r in range(taps // LANES):
+        cols = slice(r * LANES, (r + 1) * LANES)
+        row = area[r : r + 1, :]
+        w_ref[0:panels, cols] = jnp.where(panel_ref[:, cols] == ids, row, 0.0).astype(bf16)
+        w_ref[panels:rows, cols] = jnp.where(floor_ref[:, cols] == fids, row, 0.0).astype(bf16)
+
+    def sums(i, h, dst):
+        b, n = pieces[i]
+        cp, off = loads[2 * i + h]
+        cp.wait()
+        q = dot_nt(w_ref[...], pv[pl.ds(off, n * LANES), :])
+        for k in range(n):
+            dst[b + k] = q[:, k * LANES : (k + 1) * LANES]
+
+    def pair_copy(k):
+        return pltpu.make_async_remote_copy(
+            src_ref=send_p.at[k], dst_ref=recv_p.at[k], send_sem=pp_s, recv_sem=pp_r.at[k],
+            device_id={"floors": other}, device_id_type=MESH,
+        )
+
+    def up_copy(k):
+        return pltpu.make_async_remote_copy(
+            src_ref=mine.at[k, pl.ds(0, panels)], dst_ref=up.at[k], send_sem=u_s, recv_sem=u_r.at[k],
+            device_id={"taps": mate}, device_id_type=MESH,
+        )
+
+    def merge(i):
+        b, n = pieces[i]
+        for k in range(b, b + n):
+            pair_copy(k).wait_recv()
+            mine[k] = mine[k] + recv_p[k]
+
+            @pl.when(jnp.logical_not(inner))
+            def _():
+                up_copy(k).start()
+
+    for i, (b, n) in enumerate(pieces):
+        sums(i, 0, send_p)
+        if i == 0:
+
+            @pl.when(inner)
+            def _():
+                pl.semaphore_wait(barrier, 3 + ntm - 1)
+
+            @pl.when(jnp.logical_not(inner))
+            def _():
+                pl.semaphore_wait(barrier, 2 + ntm - 1)
+
+        for k in range(b, b + n):
+            pair_copy(k).start()
+        sums(i, 1, mine)
+        merge(i)
+
+    @pl.when(inner)
+    def _():
+        pl.semaphore_signal(known, inc=1, device_id={"taps": far}, device_id_type=MESH)
+
+    for cp in small[3:]:
+        cp.wait()
+    order_col[...] = jnp.transpose(jnp.broadcast_to(order_ref[...].astype(f32), (LANES, modes)))
+
+    def pick(off, n):
+        mode_ids = lax.broadcasted_iota(jnp.int32, (n, modes), 1).astype(f32)
+        return order_col[pl.ds(pl.multiple_of(off, n), n), 0:1] == mode_ids
+
+    for r in range(owners):
+        hot = pick(r * md, md).astype(f32).astype(bf16)
+        g_ref[r * md : (r + 1) * md] = dot_nt(hot, shape_ref[...]).astype(bf16)
+
+    def project(chip, n, q):
+        size = n * nc * md
+        return dot_split(g_ref[pl.ds(pl.multiple_of(chip * nc * md, size), size), :], q)
+
+    def cross_copy(k, i):
+        return pltpu.make_async_remote_copy(
+            src_ref=sx.at[k, i], dst_ref=fx.at[k, c], send_sem=x_s, recv_sem=x_r.at[k],
+            device_id={"taps": 2 * (1 - side) + i // nc, "floors": i % nc}, device_id_type=MESH,
+        )
+
+    def mate_copy(k, i):
+        return pltpu.make_async_remote_copy(
+            src_ref=si.at[k, i], dst_ref=fi.at[k, c], send_sem=i_s, recv_sem=i_r.at[k],
+            device_id={"taps": mate, "floors": i}, device_id_type=MESH,
+        )
+
+    def exchange(k):
+        return pltpu.make_async_remote_copy(
+            src_ref=sp.at[k], dst_ref=fb.at[c * tblocks + k], send_sem=e_s, recv_sem=e_r.at[k],
+            device_id={"floors": other}, device_id_type=MESH,
+        )
+
+    def keep(k, both):
+        both = both.reshape(nc, md, LANES)
+        sp[k] = jnp.where(c == 0, both[1], both[0])
+        exchange(k).start()
+        fb[c * tblocks + k] = jnp.where(c == 0, both[0], both[1])
+
+    @pl.when(inner)
+    def _():
+        for k in range(tblocks):
+            si[k] = project(mate, 1, mine[k, 0:panels]).reshape(nc, md, LANES)
+            for i in range(nc):
+                mate_copy(k, i).start()
+
+    @pl.when(jnp.logical_not(inner))
+    def _():
+        for k in range(tblocks):
+            keep(k, project(z, 1, mine[k, 0:panels]))
+
+    for k in range(tblocks):
+        part = mine[k, panels:rows]
+        for j in range(owners):
+            fls[j, :, k * LANES : (k + 1) * LANES] = part[j * fd : (j + 1) * fd]
+
+    hot_me = pick(me * md, md)
+    d = jnp.sum(jnp.where(hot_me, decay_ref[...], 0.0), axis=1, keepdims=True)
+    w = jnp.sum(jnp.where(hot_me, freq_ref[...], 0.0), axis=1, keepdims=True)
+    ls = dot_nt(fshape_ref[...], hot_me.astype(f32).astype(bf16)).astype(bf16)
+    e2 = 2.0 * d
+    poly = jnp.full_like(e2, 1.0 / 40320.0)
+    for coef in (1.0 / 5040, 1.0 / 720, 1.0 / 120, 1.0 / 24, 1.0 / 6, 0.5, 1.0):
+        poly = coef - e2 * poly
+    gain = jnp.sqrt(e2 * poly)
+    lane = lax.broadcasted_iota(jnp.int32, (md, LANES), 1)
+    ahead = (lane + 1).astype(f32)
+    mag = jnp.exp(-d * ahead)
+    t_re = mag * jnp.cos(w * ahead)
+    t_im = mag * jnp.sin(w * ahead)
+    tabs[0] = t_re
+    tabs[1] = t_im
+    hops = []
+    step = 1
+    while step < LANES:
+        i = 2 + 2 * len(hops)
+        tabs[i] = jnp.where(lane >= step, t_re[:, step - 1 : step], 0.0)
+        tabs[i + 1] = jnp.where(lane >= step, t_im[:, step - 1 : step], 0.0)
+        hops.append(step)
+        step *= 2
+
+    @pl.when(inner)
+    def _():
+        pl.semaphore_wait(known, 1)
+        pl.semaphore_signal(known, inc=1, device_id={"taps": mate}, device_id_type=MESH)
+        for k in range(tblocks):
+            up_copy(k).wait_recv()
+            total = mine[k, 0:panels] + up[k]
+            sx[k] = project(2 * (1 - side), 2, total).reshape(2 * nc, md, LANES)
+            for i in range(2 * nc):
+                cross_copy(k, i).start()
+            keep(k, project(z, 1, total))
+
+    @pl.when(jnp.logical_not(inner))
+    def _():
+        pl.semaphore_wait(known, 1)
+
+    def load_copy(k):
+        j = lax.rem(me + k, owners)
+        return pltpu.make_async_remote_copy(
+            src_ref=fls.at[j], dst_ref=flr.at[k - 1], send_sem=fl_s, recv_sem=fl_r,
+            device_id={"taps": j // nc, "floors": lax.rem(j, nc)}, device_id_type=MESH,
+        )
+
+    def load_start(k, carry):
+        load_copy(k).start()
+        return carry
+
+    lax.fori_loop(1, owners, load_start, 0)
+
+    def at_rest(blk, force):
+        re = gain * force
+        im = None
+        for i, step in enumerate(hops):
+            a, b = tabs[2 + 2 * i], tabs[3 + 2 * i]
+            rr = pltpu.roll(re, step, 1)
+            if im is None:
+                re, im = re + a * rr, b * rr
+            else:
+                ri = pltpu.roll(im, step, 1)
+                re, im = re + a * rr - b * ri, im + a * ri + b * rr
+        loc[blk] = re
+        loc_im[blk] = im
+
+    for k in range(tblocks):
+        exchange(k).wait_recv()
+
+        @pl.when(jnp.logical_not(inner))
+        def _():
+            pltpu.make_async_copy(fi.at[k], fi.at[k], i_r.at[k]).wait()
+            for h in range(nc):
+                fb[h * tblocks + k] = fb[h * tblocks + k] + fi[k, h]
+
+        pltpu.make_async_copy(fx.at[k], fx.at[k], x_r.at[k]).wait()
+        for h in range(nc):
+            at_rest(h * tblocks + k, fb[h * tblocks + k] + fx[k, h])
+
+    nb = time_dev // LANES
+    end_re = [loc[blk][:, LANES - 1 :] for blk in range(nb)]
+    end_im = [loc_im[blk][:, LANES - 1 :] for blk in range(nb)]
+    zb_re, zb_im = t_re[:, LANES - 1 :], t_im[:, LANES - 1 :]
+    s_re, s_im = end_re[0], end_im[0]
+    for blk in range(1, nb):
+        s_re, s_im = (
+            zb_re * s_re - zb_im * s_im + end_re[blk],
+            zb_im * s_re + zb_re * s_im + end_im[blk],
+        )
+
+    def state_copy(to, src):
+        return pltpu.make_async_remote_copy(
+            src_ref=st_send, dst_ref=st_recv.at[src], send_sem=t_s.at[to], recv_sem=t_r.at[src],
+            device_id={"tm": to}, device_id_type=MESH,
+        )
+
+    st_send[...] = jnp.where(lane == 0, s_re, s_im)
+    in_re = jnp.zeros((md, 1), f32)
+    in_im = jnp.zeros((md, 1), f32)
+    if ntm > 1:
+        for to in range(1, ntm):
+
+            @pl.when(x < to)
+            def _():
+                state_copy(to, jnp.minimum(x, ntm - 2)).start()
+
+        for src in range(ntm - 1):
+
+            @pl.when(x > src)
+            def _():
+                state_copy(lax.rem(x + 1, ntm), src).wait_recv()
+
+            @pl.when(x <= src)
+            def _():
+                st_recv[src] = jnp.zeros_like(st_send)
+
+            got_re, got_im = st_recv[src][:, 0:1], st_recv[src][:, 1:2]
+            if ntm == 2:
+                in_re, in_im = got_re, got_im
+                continue
+            length = (jnp.maximum(x - 1 - src, 0) * time_dev).astype(f32)
+            pm = jnp.exp(-d * length)
+            pr, pi = pm * jnp.cos(w * length), pm * jnp.sin(w * length)
+            in_re = in_re + pr * got_re - pi * got_im
+            in_im = in_im + pi * got_re + pr * got_im
+
+    t_re, t_im = tabs[0], tabs[1]
+    for blk in range(nb):
+        y = loc[blk] + t_re * in_re - t_im * in_im
+        cols = slice(blk * LANES, (blk + 1) * LANES)
+        y_ref[:, cols] = y
+        in_re, in_im = (
+            zb_re * in_re - zb_im * in_im + end_re[blk],
+            zb_im * in_re + zb_re * in_im + end_im[blk],
+        )
+    part = dot_split(ls, y_ref[...])
+    for j in range(owners):
+        fs[j] = part[j * fd : (j + 1) * fd]
+
+    def motion_copy(k):
+        j = lax.rem(me + k, owners)
+        return pltpu.make_async_remote_copy(
+            src_ref=fs.at[j], dst_ref=fr.at[k - 1], send_sem=f_s, recv_sem=f_r,
+            device_id={"taps": j // nc, "floors": lax.rem(j, nc)}, device_id_type=MESH,
+        )
+
+    def motion_start(k, carry):
+        motion_copy(k).start()
+        return carry
+
+    lax.fori_loop(1, owners, motion_start, 0)
+
+    def drain(ref, sem):
+        pltpu.make_async_copy(ref, ref, sem).wait()
+
+    drain(flr, fl_r)
+    load_scale = (floors / (taps * owners)) ** 0.5
+    halves = []
+    for h in range(nc):
+        total = jnp.where(c == h, fls[me], 0.0)
+        for k in range(1, owners):
+            src = lax.rem(me + owners - k, owners)
+            total = total + jnp.where(lax.rem(src, nc) == h, flr[k - 1], 0.0)
+        halves.append(total * load_scale)
+    for h in range(nc):
+        fl_ref[:, h * th : (h + 1) * th] = halves[h]
+
+    drain(send_p, pp_s)
+
+    @pl.when(inner)
+    def _():
+        drain(si, i_s)
+        drain(sx, x_s)
+
+    @pl.when(jnp.logical_not(inner))
+    def _():
+        drain(up, u_s)
+
+    drain(sp, e_s)
+    drain(flr, fl_s)
+    for to in range(1, ntm):
+
+        @pl.when(x < to)
+        def _():
+            state_copy(to, jnp.minimum(x, ntm - 2)).wait_send()
+
+    drain(fr, f_r)
+    total = fs[me]
+    for k in range(1, owners):
+        total = total + fr[k - 1]
+    fm_ref[...] = total
+    drain(fr, f_s)
+
+
 def write_out(y, fm, fl, y_out, fm_out, fl_out, sem):
     copies = [
         pltpu.make_async_copy(src, dst, sem.at[i])
@@ -406,12 +789,79 @@
     md, fd = modes // owners, floors // owners
     nch = th // LANES * splits
     xrows = md + -(-fd // 8) * 8
-    chunk = pltpu.VMEM((nch, rows // splits, LANES), jnp.float32)
     vmem = pl.BlockSpec(memory_space=pltpu.VMEM)
     dma = pltpu.SemaphoreType.DMA
     f32 = jnp.float32
+    tb, nb = th // LANES, time_dev // LANES
+    inputs = [
+        pltpu.VMEM((taps // LANES, LANES), jnp.bfloat16),
+        pltpu.VMEM((1, taps), jnp.int32),
+        pltpu.VMEM((1, taps), jnp.int32),
+        pltpu.VMEM(panel_shape.shape, jnp.bfloat16),
+        pltpu.VMEM(floor_shape.shape, jnp.bfloat16),
+        pltpu.VMEM((1, modes), jnp.int32),
+        pltpu.VMEM((1, modes), f32),
+        pltpu.VMEM((1, modes), f32),
+        pltpu.VMEM((modes, LANES), f32),
+        pltpu.VMEM((time_dev, taps), jnp.bfloat16),
+        pltpu.VMEM((rows, taps), jnp.bfloat16),
+    ]
+    response = [
+        pltpu.VMEM((16, md, LANES), f32),
+        pltpu.VMEM((nb, md, LANES), f32),
+        pltpu.VMEM((nb, md, LANES), f32),
+        pltpu.VMEM((md, LANES), f32),
+        pltpu.VMEM((max(ntm - 1, 1), md, LANES), f32),
+    ]
+    if nz == 4 and nc == 2 and tb % 2 == 0:
+        block = pltpu.VMEM((tb, rows, LANES), f32)
+        pieces = ((0, 1), (1, 1)) + tuple((b, 2) for b in range(2, tb, 2))
+        body = functools.partial(two_stage, (nz, nc, ntm, pieces))
+        scratch = (
+            inputs
+            + [pltpu.VMEM((modes, panels), jnp.bfloat16), block, block, block]
+            + [
+                pltpu.VMEM((tb, panels, LANES), f32),
+                pltpu.VMEM((tb, 2 * nc, md, LANES), f32),
+                pltpu.VMEM((tb, nc, md, LANES), f32),
+                pltpu.VMEM((tb, nc, md, LANES), f32),
+                pltpu.VMEM((tb, nc, md, LANES), f32),
+                pltpu.VMEM((tb, md, LANES), f32),
+                pltpu.VMEM((nb, md, LANES), f32),
+            ]
+            + response
+            + [
+                pltpu.VMEM((owners, fd, th), f32),
+                pltpu.VMEM((owners - 1, fd, th), f32),
+                pltpu.VMEM((owners, fd, time_dev), f32),
+                pltpu.VMEM((owners - 1, fd, time_dev), f32),
+                dma((8,)), dma((2 * len(pieces),)),
+                dma(()), dma((tb,)), dma(()), dma((tb,)), dma(()), dma((tb,)), dma(()), dma((tb,)),
+                dma(()), dma((tb,)), dma(()), dma(()), dma((ntm,)), dma((ntm,)), dma(()), dma(()),
+                pltpu.SemaphoreType.REGULAR,
+            ]
+        )
+    else:
+        chunk = pltpu.VMEM((nch, rows // splits, LANES), f32)
+        body = functools.partial(kernel, (nz, nc, ntm, splits))
+        scratch = (
+            inputs
+            + [chunk] * 7
+            + [pltpu.VMEM((tb, xrows, LANES), f32), pltpu.VMEM((nb, xrows, LANES), f32)]
+            + response
+            + [
+                pltpu.VMEM((owners, fd, time_dev), f32),
+                pltpu.VMEM((owners, fd, time_dev), f32),
+                dma((8,)),
+                dma((2 * (th // min(256, th)),)),
+                dma((nch,)), dma((nch,)), dma((nch,)), dma((nch,)), dma((nch,)), dma((nch,)),
+                dma((tb,)), dma((tb,)),
+                dma((ntm,)), dma((ntm,)),
+                dma((owners,)), dma((owners,)),
+            ]
+        )
     out = pl.pallas_call(
-        functools.partial(kernel, (nz, nc, ntm, splits)),
+        body,
         out_shape=(
             pltpu.VMEM((md, time_dev), f32),
             pltpu.VMEM((fd, time_dev), f32),
@@ -419,35 +869,7 @@
         ),
         in_specs=[pl.BlockSpec(memory_space=pltpu.HBM)] * 9,
         out_specs=(vmem,) * 3,
-        scratch_shapes=[
-            pltpu.VMEM((taps // LANES, LANES), jnp.bfloat16),
-            pltpu.VMEM((1, taps), jnp.int32),
-            pltpu.VMEM((1, taps), jnp.int32),
-            pltpu.VMEM(panel_shape.shape, jnp.bfloat16),
-            pltpu.VMEM(floor_shape.shape, jnp.bfloat16),
-            pltpu.VMEM((1, modes), jnp.int32),
-            pltpu.VMEM((1, modes), f32),
-            pltpu.VMEM((1, modes), f32),
-            pltpu.VMEM((modes, LANES), f32),
-            pltpu.VMEM((time_dev, taps), jnp.bfloat16),
-            pltpu.VMEM((rows, taps), jnp.bfloat16),
-            chunk, chunk, chunk, chunk, chunk, chunk, chunk,
-            pltpu.VMEM((th // LANES, xrows, LANES), f32),
-            pltpu.VMEM((time_dev // LANES, xrows, LANES), f32),
-            pltpu.VMEM((16, md, LANES), f32),
-            pltpu.VMEM((time_dev // LANES, md, LANES), f32),
-            pltpu.VMEM((time_dev // LANES, md, LANES), f32),
-            pltpu.VMEM((md, LANES), f32),
-            pltpu.VMEM((max(ntm - 1, 1), md, LANES), f32),
-            pltpu.VMEM((owners, fd, time_dev), f32),
-            pltpu.VMEM((owners, fd, time_dev), f32),
-            dma((8,)),
-            dma((2 * (th // min(256, th)),)),
-            dma((nch,)), dma((nch,)), dma((nch,)), dma((nch,)), dma((nch,)), dma((nch,)),
-            dma((th // LANES,)), dma((th // LANES,)),
-            dma((ntm,)), dma((ntm,)),
-            dma((owners,)), dma((owners,)),
-        ],
+        scratch_shapes=scratch,
         compiler_params=pltpu.CompilerParams(
             collective_id=0, has_side_effects=True, vmem_limit_bytes=VMEM_LIMIT
         ),

time: 37.6 us -> 32.9 us (0.87)
  the two profiles are of different devices: /device:TPU:7 before, /device:TPU:3 now
where the time goes in v2:
time: 32.9 us; the launch traced here: 32.8 us
  Pallas kernels  32.1 us (98%)
  between operations  0.64 us (2%)
    pallas_call x1, Pallas kernels, on_device(): pl.pallas_call(body, out_shape=(pltpu.VMEM((md, time_dev), f32), pltpu.VM...  31.4 us
    pallas_call x1, Pallas kernels, on_device(): pl.pallas_call(write_out, out_shape=tuple((jax.ShapeDtypeStruct(o.shape,...  0.74 us

profile of v2, /device:TPU:3, one launch (start us, length us, event | category | flops | bytes accessed | tf_op | source)
XLA Modules:
  0.0 32.8 jit_solution(10633085963693896647)
XLA Ops:
  0.6 31.4 %shard_map.112 = (f32[64,1024]{1,0:T(8,128)S(1)}, f32[2,1024]{1,0:T(2,128)S(1)}, f32[2,1024]{1,0:T(2,128)S(1)}) custom-call(bf16[1024,2048]{1,0:T(8,128)(2,1)} %p_hbm.1, bf16[16,128]{1,0:T(8,128)(2,1)} %bitcast.8, s32[1,2048]{1,0:T(1,128)} %bitcast.6, s32[1,2048]{1,0:T(1,128)} %bitcast.7, bf16[256,512]{1,0:T(8,128)(2,1)} %shape_h.1, ...), custom_call_target="tpu_custom_call" | custom-call | tf_op jit(solution)/shard_map/pallas_call | solution.py:863
  32.0 0.7 %shard_map.113 = (f32[64,1024]{1,0:T(8,128)}, f32[2,1024]{1,0:T(2,128)}, f32[2,1024]{1,0:T(2,128)}) custom-call(f32[64,1024]{1,0:T(8,128)S(1)} %get-tuple-element.6.y, f32[2,1024]{1,0:T(2,128)S(1)} %get-tuple-element.7.fm, f32[2,1024]{1,0:T(2,128)S(1)} %get-tuple-element.8.fl), custom_call_target="tpu_custom_call" | custom-call | tf_op jit(solution)/shard_map/pallas_call | solution.py:892

commit v3 on v2

--- a/solution.py
+++ b/solution.py
@@ -386,9 +386,9 @@
     p_hbm, area_h, panel_h, floor_h, shape_h, fshape_h, order_h, decay_h, freq_h,
     y_ref, fm_ref, fl_ref,
     area_ref, panel_ref, floor_ref, shape_ref, fshape_ref, order_ref, decay_ref, freq_ref, order_col,
-    pv, w_ref, g_ref, send_p, recv_p, mine, up, sx, fx, si, fi, sp, fb, tabs, loc, loc_im, st_send, st_recv,
-    fls, flr, fs, fr,
-    in_sem, p_sem, pp_s, pp_r, u_s, u_r, x_s, x_r, i_s, i_r, e_s, e_r, fl_s, fl_r, t_s, t_r, f_s, f_r, known,
+    pv, w_ref, g_ref, send_p, recv_p, mine, up, sx, fx, si, fi, sp, fb, tabs, loc, loc_im, ends, st_send, st_recv,
+    fls, flr, fs, fr, cs, cr,
+    in_sem, p_sem, pp_s, pp_r, u_s, u_r, x_s, x_r, i_s, i_r, e_s, e_r, fl_s, fl_r, t_s, t_r, f_s, f_r, c_s, c_r, known,
 ):
     nz, nc, ntm, pieces = cfg
     owners = nz * nc
@@ -577,21 +577,34 @@
     for coef in (1.0 / 5040, 1.0 / 720, 1.0 / 120, 1.0 / 24, 1.0 / 6, 0.5, 1.0):
         poly = coef - e2 * poly
     gain = jnp.sqrt(e2 * poly)
+    nb = time_dev // LANES
     lane = lax.broadcasted_iota(jnp.int32, (md, LANES), 1)
-    ahead = (lane + 1).astype(f32)
-    mag = jnp.exp(-d * ahead)
-    t_re = mag * jnp.cos(w * ahead)
-    t_im = mag * jnp.sin(w * ahead)
-    tabs[0] = t_re
-    tabs[1] = t_im
-    hops = []
-    step = 1
-    while step < LANES:
-        i = 2 + 2 * len(hops)
-        tabs[i] = jnp.where(lane >= step, t_re[:, step - 1 : step], 0.0)
-        tabs[i + 1] = jnp.where(lane >= step, t_im[:, step - 1 : step], 0.0)
-        hops.append(step)
-        step *= 2
+    steps = lane.astype(f32)
+    cos, sin = jnp.cos(w * steps), jnp.sin(w * steps)
+    grow = gain * jnp.exp(d * steps)
+    decay = jnp.exp(-d * steps)
+    t_re, t_im = decay * cos, decay * sin
+    for i, table in enumerate((t_re, t_im, grow * cos, -grow * sin)):
+        tabs[i] = table
+    upto = lax.broadcasted_iota(jnp.int32, (LANES, 2 * LANES), 0) <= lax.broadcasted_iota(
+        jnp.int32, (LANES, 2 * LANES), 1
+    )
+    upto = upto.astype(f32).astype(bf16)
+
+    def times(a_re, a_im, b_re, b_im):
+        return a_re * b_re - a_im * b_im, a_re * b_im + a_im * b_re
+
+    def wide(v):
+        return jnp.broadcast_to(v, (md, LANES))
+
+    last = LANES - 1
+    for i, table in enumerate(
+        times(t_re[:, 1:2], t_im[:, 1:2], t_re[:, last:], t_im[:, last:])
+    ):
+        tabs[4 + i] = wide(table)
+
+    def turn(re, im):
+        return times(tabs[4], tabs[5], re, im)
 
     @pl.when(inner)
     def _():
@@ -622,19 +635,34 @@
 
     lax.fori_loop(1, owners, load_start, 0)
 
-    def at_rest(blk, force):
-        re = gain * force
-        im = None
-        for i, step in enumerate(hops):
-            a, b = tabs[2 + 2 * i], tabs[3 + 2 * i]
-            rr = pltpu.roll(re, step, 1)
-            if im is None:
-                re, im = re + a * rr, b * rr
-            else:
-                ri = pltpu.roll(im, step, 1)
-                re, im = re + a * rr - b * ri, im + a * ri + b * rr
-        loc[blk] = re
-        loc_im[blk] = im
+    def prefix(blks):
+        parts = [fb[blk] * tabs[2 + i] for blk in blks for i in range(2)]
+        v = jnp.concatenate(parts, axis=0)
+        hi = v.astype(bf16)
+        lo = (v - hi.astype(f32)).astype(bf16)
+        v = jnp.dot(hi, upto, preferred_element_type=f32) + jnp.dot(
+            lo, upto, preferred_element_type=f32
+        )
+        for n, blk in enumerate(blks):
+            for i, dst in enumerate((loc, loc_im)):
+                part = v[(2 * n + i) * md : (2 * n + i + 1) * md]
+                dst[blk] = part[:, :LANES]
+                ends[blk, i] = part[:, LANES:]
+
+    def response(blk, re, im):
+        return tabs[0] * (loc[blk] + re) - tabs[1] * (loc_im[blk] + im)
+
+    def state_copy(to, src):
+        return pltpu.make_async_remote_copy(
+            src_ref=st_send, dst_ref=st_recv.at[src], send_sem=t_s.at[to], recv_sem=t_r.at[src],
+            device_id={"tm": to}, device_id_type=MESH,
+        )
+
+    def carry_copy(to, src, j):
+        return pltpu.make_async_remote_copy(
+            src_ref=cs.at[to - 1, j], dst_ref=cr.at[src, me], send_sem=c_s.at[to], recv_sem=c_r.at[src],
+            device_id={"tm": to, "taps": j // nc, "floors": j % nc}, device_id_type=MESH,
+        )
 
     for k in range(tblocks):
         exchange(k).wait_recv()
@@ -647,65 +675,17 @@
 
         pltpu.make_async_copy(fx.at[k], fx.at[k], x_r.at[k]).wait()
         for h in range(nc):
-            at_rest(h * tblocks + k, fb[h * tblocks + k] + fx[k, h])
-
-    nb = time_dev // LANES
-    end_re = [loc[blk][:, LANES - 1 :] for blk in range(nb)]
-    end_im = [loc_im[blk][:, LANES - 1 :] for blk in range(nb)]
-    zb_re, zb_im = t_re[:, LANES - 1 :], t_im[:, LANES - 1 :]
-    s_re, s_im = end_re[0], end_im[0]
-    for blk in range(1, nb):
-        s_re, s_im = (
-            zb_re * s_re - zb_im * s_im + end_re[blk],
-            zb_im * s_re + zb_re * s_im + end_im[blk],
-        )
-
-    def state_copy(to, src):
-        return pltpu.make_async_remote_copy(
-            src_ref=st_send, dst_ref=st_recv.at[src], send_sem=t_s.at[to], recv_sem=t_r.at[src],
-            device_id={"tm": to}, device_id_type=MESH,
-        )
-
-    st_send[...] = jnp.where(lane == 0, s_re, s_im)
-    in_re = jnp.zeros((md, 1), f32)
-    in_im = jnp.zeros((md, 1), f32)
-    if ntm > 1:
-        for to in range(1, ntm):
-
-            @pl.when(x < to)
-            def _():
-                state_copy(to, jnp.minimum(x, ntm - 2)).start()
-
-        for src in range(ntm - 1):
-
-            @pl.when(x > src)
-            def _():
-                state_copy(lax.rem(x + 1, ntm), src).wait_recv()
-
-            @pl.when(x <= src)
-            def _():
-                st_recv[src] = jnp.zeros_like(st_send)
-
-            got_re, got_im = st_recv[src][:, 0:1], st_recv[src][:, 1:2]
-            if ntm == 2:
-                in_re, in_im = got_re, got_im
-                continue
-            length = (jnp.maximum(x - 1 - src, 0) * time_dev).astype(f32)
-            pm = jnp.exp(-d * length)
-            pr, pi = pm * jnp.cos(w * length), pm * jnp.sin(w * length)
-            in_re = in_re + pr * got_re - pi * got_im
-            in_im = in_im + pi * got_re + pr * got_im
-
-    t_re, t_im = tabs[0], tabs[1]
+            fb[h * tblocks + k] = fb[h * tblocks + k] + fx[k, h]
+        prefix([h * tblocks + k for h in range(nc)])
+
+    re, im = jnp.zeros((md, LANES), f32), jnp.zeros((md, LANES), f32)
+    ys = []
     for blk in range(nb):
-        y = loc[blk] + t_re * in_re - t_im * in_im
-        cols = slice(blk * LANES, (blk + 1) * LANES)
-        y_ref[:, cols] = y
-        in_re, in_im = (
-            zb_re * in_re - zb_im * in_im + end_re[blk],
-            zb_im * in_re + zb_re * in_im + end_im[blk],
-        )
-    part = dot_split(ls, y_ref[...])
+        ys.append(response(blk, re, im))
+        re, im = turn(ends[blk, 0] + re, ends[blk, 1] + im)
+    y = jnp.concatenate(ys, axis=1)
+    y_ref[...] = y
+    part = dot_split(ls, y)
     for j in range(owners):
         fs[j] = part[j * fd : (j + 1) * fd]
 
@@ -721,6 +701,57 @@
         return carry
 
     lax.fori_loop(1, owners, motion_start, 0)
+    s_re, s_im = re, im
+    for to in range(1, ntm):
+
+        @pl.when(x < to)
+        def _():
+            src = jnp.minimum(x, ntm - 2)
+            re, im = s_re, s_im
+            if ntm > 2:
+                gap = ((to - 1 - x) * time_dev).astype(f32)
+                pm = jnp.exp(-d * gap)
+                re, im = times(pm * jnp.cos(w * gap), pm * jnp.sin(w * gap), re, im)
+            ys = []
+            for blk in range(nb):
+                ys.append(tabs[0] * re - tabs[1] * im)
+                re, im = turn(re, im)
+            part = dot_split(ls, jnp.concatenate(ys, axis=1))
+            for j in range(owners):
+                cs[to - 1, j] = part[j * fd : (j + 1) * fd]
+            for j in range(owners):
+                carry_copy(to, src, j).start()
+            st_send[...] = jnp.where(lane == 0, s_re, s_im)
+            state_copy(to, src).start()
+
+    in_re = jnp.zeros((md, LANES), f32)
+    in_im = jnp.zeros((md, LANES), f32)
+    for src in range(ntm - 1):
+
+        @pl.when(x > src)
+        def _():
+            state_copy(lax.rem(x + 1, ntm), src).wait_recv()
+
+        @pl.when(x <= src)
+        def _():
+            st_recv[src] = jnp.zeros_like(st_send)
+
+        got_re, got_im = wide(st_recv[src][:, 0:1]), wide(st_recv[src][:, 1:2])
+        if ntm == 2:
+            in_re, in_im = got_re, got_im
+            continue
+        length = (jnp.maximum(x - 1 - src, 0) * time_dev).astype(f32)
+        pm = jnp.exp(-d * length)
+        got_re, got_im = times(pm * jnp.cos(w * length), pm * jnp.sin(w * length), got_re, got_im)
+        in_re, in_im = in_re + got_re, in_im + got_im
+
+    @pl.when(x > 0)
+    def _():
+        re, im = in_re, in_im
+        for blk in range(nb):
+            cols = slice(blk * LANES, (blk + 1) * LANES)
+            y_ref[:, cols] = y_ref[:, cols] + tabs[0] * re - tabs[1] * im
+            re, im = turn(re, im)
 
     def drain(ref, sem):
         pltpu.make_async_copy(ref, ref, sem).wait()
@@ -762,6 +793,21 @@
         total = total + fr[k - 1]
     fm_ref[...] = total
     drain(fr, f_s)
+    for src in range(ntm - 1):
+
+        @pl.when(x > src)
+        def _():
+            drain(cr.at[src], c_r.at[src])
+            carried = fm_ref[...]
+            for j in range(owners):
+                carried = carried + cr[src, j]
+            fm_ref[...] = carried
+
+    for to in range(1, ntm):
+
+        @pl.when(x < to)
+        def _():
+            drain(cs.at[to - 1], c_s.at[to])
 
 
 def write_out(y, fm, fl, y_out, fm_out, fl_out, sem):
@@ -829,15 +875,20 @@
                 pltpu.VMEM((tb, md, LANES), f32),
                 pltpu.VMEM((nb, md, LANES), f32),
             ]
-            + response
+            + response[:3]
+            + [pltpu.VMEM((nb, 2, md, LANES), f32)]
+            + response[3:]
             + [
                 pltpu.VMEM((owners, fd, th), f32),
                 pltpu.VMEM((owners - 1, fd, th), f32),
                 pltpu.VMEM((owners, fd, time_dev), f32),
                 pltpu.VMEM((owners - 1, fd, time_dev), f32),
+                pltpu.VMEM((max(ntm - 1, 1), owners, fd, time_dev), f32),
+                pltpu.VMEM((max(ntm - 1, 1), owners, fd, time_dev), f32),
                 dma((8,)), dma((2 * len(pieces),)),
                 dma(()), dma((tb,)), dma(()), dma((tb,)), dma(()), dma((tb,)), dma(()), dma((tb,)),
                 dma(()), dma((tb,)), dma(()), dma(()), dma((ntm,)), dma((ntm,)), dma(()), dma(()),
+                dma((ntm,)), dma((ntm,)),
                 pltpu.SemaphoreType.REGULAR,
             ]
         )

time: 32.9 us -> 30.9 us (0.939)
  the two profiles are of different devices: /device:TPU:3 before, /device:TPU:0 now
where the time goes in v3:
time: 30.9 us; the launch traced here: 30.7 us
  Pallas kernels  30.1 us (97%)
  between operations  0.64 us (2%)
    pallas_call x1, Pallas kernels, on_device(): pl.pallas_call(body, out_shape=(pltpu.VMEM((md, time_dev), f32), pltpu.VM...  29.4 us
    pallas_call x1, Pallas kernels, on_device(): pl.pallas_call(write_out, out_shape=tuple((jax.ShapeDtypeStruct(o.shape,...  0.74 us

profile of v3, /device:TPU:0, one launch (start us, length us, event | category | flops | bytes accessed | tf_op | source)
XLA Modules:
  0.0 30.7 jit_solution(11305447502129073462)
XLA Ops:
  0.6 29.4 %shard_map.112 = (f32[64,1024]{1,0:T(8,128)S(1)}, f32[2,1024]{1,0:T(2,128)S(1)}, f32[2,1024]{1,0:T(2,128)S(1)}) custom-call(bf16[1024,2048]{1,0:T(8,128)(2,1)} %p_hbm.1, bf16[16,128]{1,0:T(8,128)(2,1)} %bitcast.8, s32[1,2048]{1,0:T(1,128)} %bitcast.6, s32[1,2048]{1,0:T(1,128)} %bitcast.7, bf16[256,512]{1,0:T(8,128)(2,1)} %shape_h.1, ...), custom_call_target="tpu_custom_call" | custom-call | tf_op jit(solution)/shard_map/pallas_call | solution.py:914
  30.0 0.7 %shard_map.113 = (f32[64,1024]{1,0:T(8,128)}, f32[2,1024]{1,0:T(2,128)}, f32[2,1024]{1,0:T(2,128)}) custom-call(f32[64,1024]{1,0:T(8,128)S(1)} %get-tuple-element.6.y, f32[2,1024]{1,0:T(2,128)S(1)} %get-tuple-element.7.fm, f32[2,1024]{1,0:T(2,128)S(1)} %get-tuple-element.8.fl), custom_call_target="tpu_custom_call" | custom-call | tf_op jit(solution)/shard_map/pallas_call | solution.py:943

commit v4 on v3

--- a/solution.py
+++ b/solution.py
@@ -10,6 +10,7 @@
 MESH = pl.DeviceIdType.MESH
 LANES = 128
 LAG = 2
+CUT = 2
 VMEM_LIMIT = 32 * 1024 * 1024
 NT = (((1,), (1,)), ((), ()))
 
@@ -386,11 +387,11 @@
     p_hbm, area_h, panel_h, floor_h, shape_h, fshape_h, order_h, decay_h, freq_h,
     y_ref, fm_ref, fl_ref,
     area_ref, panel_ref, floor_ref, shape_ref, fshape_ref, order_ref, decay_ref, freq_ref, order_col,
-    pv, w_ref, g_ref, send_p, recv_p, mine, up, sx, fx, si, fi, sp, fb, tabs, loc, loc_im, ends, st_send, st_recv,
+    pv, w_ref, g_ref, send_p, recv_p, mine, mp, up, sx, fx, si, fi, sp, fb, tabs, loc, loc_im, ends, st_send, st_recv,
     fls, flr, fs, fr, cs, cr,
     in_sem, p_sem, pp_s, pp_r, u_s, u_r, x_s, x_r, i_s, i_r, e_s, e_r, fl_s, fl_r, t_s, t_r, f_s, f_r, c_s, c_r, known,
 ):
-    nz, nc, ntm, pieces = cfg
+    nz, nc, ntm, cut = cfg
     owners = nz * nc
     z = lax.axis_index("taps")
     c = lax.axis_index("floors")
@@ -401,7 +402,8 @@
     mate = z + 1 - 2 * lax.rem(z, 2)
     far = nz - 1 - z
     inner = jnp.logical_or(z == 1, z == 2)
-    time_dev, taps = pv.shape
+    time_dev = y_ref.shape[1]
+    taps = w_ref.shape[1]
     panels, modes = shape_ref.shape
     floors = fshape_ref.shape[0]
     rows = panels + floors
@@ -423,15 +425,14 @@
     ]
     for cp in small[:3]:
         cp.start()
-    loads = []
-    for i, (b, n) in enumerate(pieces):
+    for k in range(tblocks):
         for h, half in enumerate((other, c)):
-            off = pl.multiple_of(half * th + b * LANES, LANES)
-            cp = pltpu.make_async_copy(
-                p_hbm.at[pl.ds(off, n * LANES)], pv.at[pl.ds(off, n * LANES)], p_sem.at[2 * i + h]
-            )
-            cp.start()
-            loads.append((cp, off))
+            off = pl.multiple_of(half * th + k * LANES, LANES)
+            pltpu.make_async_copy(
+                p_hbm.at[pl.ds(off, LANES)],
+                pv.at[k, pl.ds(h * LANES, LANES)],
+                p_sem.at[k + 1 if k + h else 0],
+            ).start()
     for cp in small[3:]:
         cp.start()
 
@@ -460,13 +461,14 @@
         w_ref[0:panels, cols] = jnp.where(panel_ref[:, cols] == ids, row, 0.0).astype(bf16)
         w_ref[panels:rows, cols] = jnp.where(floor_ref[:, cols] == fids, row, 0.0).astype(bf16)
 
-    def sums(i, h, dst):
-        b, n = pieces[i]
-        cp, off = loads[2 * i + h]
-        cp.wait()
-        q = dot_nt(w_ref[...], pv[pl.ds(off, n * LANES), :])
-        for k in range(n):
-            dst[b + k] = q[:, k * LANES : (k + 1) * LANES]
+    def sums(k):
+        loaded(pv.at[k], k + 1)
+        q = dot_nt(w_ref[...], pv[k])
+        send_p[k] = q[:, :LANES]
+        mine[k] = q[:, LANES:]
+
+    def loaded(ref, i):
+        pltpu.make_async_copy(ref, ref, p_sem.at[i]).wait()
 
     def pair_copy(k):
         return pltpu.make_async_remote_copy(
@@ -474,69 +476,68 @@
             device_id={"floors": other}, device_id_type=MESH,
         )
 
-    def up_copy(k):
-        return pltpu.make_async_remote_copy(
-            src_ref=mine.at[k, pl.ds(0, panels)], dst_ref=up.at[k], send_sem=u_s, recv_sem=u_r.at[k],
+    def up_copy(i):
+        return pltpu.make_async_remote_copy(
+            src_ref=mp.at[i], dst_ref=up.at[i], send_sem=u_s, recv_sem=u_r.at[i],
             device_id={"taps": mate}, device_id_type=MESH,
         )
 
-    def merge(i):
-        b, n = pieces[i]
-        for k in range(b, b + n):
-            pair_copy(k).wait_recv()
-            mine[k] = mine[k] + recv_p[k]
+    width = LANES // cut
+
+    def moved(v, groups):
+        shift = groups * width % LANES
+        return pltpu.roll(v, shift, 1) if shift else v
+
+    def packed(parts, j):
+        group = lax.broadcasted_iota(jnp.int32, parts[0].shape, 1) // width
+        out = moved(parts[0], -j)
+        for g in range(1, cut):
+            out = jnp.where(group == g, moved(parts[g], g - j), out)
+        return out
+
+    def split(v):
+        n = v.shape[0] // cut
+        return [v[g * n : (g + 1) * n] for g in range(cut)]
+
+    def merge(k):
+        pair_copy(k).wait_recv()
+        total = mine[k] + recv_p[k]
+        mine[k] = total
+        for j in range(cut):
+            mp[k * cut + j] = packed(split(total[:panels]), j)
 
             @pl.when(jnp.logical_not(inner))
             def _():
-                up_copy(k).start()
-
-    for i, (b, n) in enumerate(pieces):
-        sums(i, 0, send_p)
-        if i == 0:
-
-            @pl.when(inner)
-            def _():
-                pl.semaphore_wait(barrier, 3 + ntm - 1)
-
-            @pl.when(jnp.logical_not(inner))
-            def _():
-                pl.semaphore_wait(barrier, 2 + ntm - 1)
-
-        for k in range(b, b + n):
-            pair_copy(k).start()
-        sums(i, 1, mine)
-        merge(i)
-
-    @pl.when(inner)
-    def _():
-        pl.semaphore_signal(known, inc=1, device_id={"taps": far}, device_id_type=MESH)
-
-    for cp in small[3:]:
-        cp.wait()
-    order_col[...] = jnp.transpose(jnp.broadcast_to(order_ref[...].astype(f32), (LANES, modes)))
+                up_copy(k * cut + j).start()
 
     def pick(off, n):
         mode_ids = lax.broadcasted_iota(jnp.int32, (n, modes), 1).astype(f32)
         return order_col[pl.ds(pl.multiple_of(off, n), n), 0:1] == mode_ids
 
-    for r in range(owners):
-        hot = pick(r * md, md).astype(f32).astype(bf16)
-        g_ref[r * md : (r + 1) * md] = dot_nt(hot, shape_ref[...]).astype(bf16)
+    def prepare():
+        for cp in small[3:]:
+            cp.wait()
+        order_col[...] = jnp.transpose(jnp.broadcast_to(order_ref[...].astype(f32), (LANES, modes)))
+
+        n = modes // 2
+        for r in range(2):
+            hot = pick(r * n, n).astype(f32).astype(bf16)
+            g_ref[r * n : (r + 1) * n] = dot_nt(hot, shape_ref[...]).astype(bf16)
 
     def project(chip, n, q):
         size = n * nc * md
         return dot_split(g_ref[pl.ds(pl.multiple_of(chip * nc * md, size), size), :], q)
 
+    def mate_copy(k, i):
+        return pltpu.make_async_remote_copy(
+            src_ref=si.at[k, i], dst_ref=fi.at[k, c], send_sem=i_s, recv_sem=i_r.at[k],
+            device_id={"taps": mate, "floors": i}, device_id_type=MESH,
+        )
+
     def cross_copy(k, i):
         return pltpu.make_async_remote_copy(
             src_ref=sx.at[k, i], dst_ref=fx.at[k, c], send_sem=x_s, recv_sem=x_r.at[k],
             device_id={"taps": 2 * (1 - side) + i // nc, "floors": i % nc}, device_id_type=MESH,
-        )
-
-    def mate_copy(k, i):
-        return pltpu.make_async_remote_copy(
-            src_ref=si.at[k, i], dst_ref=fi.at[k, c], send_sem=i_s, recv_sem=i_r.at[k],
-            device_id={"taps": mate, "floors": i}, device_id_type=MESH,
         )
 
     def exchange(k):
@@ -551,12 +552,73 @@
         exchange(k).start()
         fb[c * tblocks + k] = jnp.where(c == 0, both[0], both[1])
 
+    def across(k):
+        got = []
+        for j in range(cut):
+            n = k * cut + j
+            up_copy(n).wait_recv()
+            total = mp[n] + up[n]
+            got.append(total)
+            total = jnp.concatenate([moved(total, j - g) for g in range(cut)], axis=0)
+            f = project(2 * (1 - side), 2, total).reshape(2 * nc, cut, md // cut, LANES)
+            f = packed([f[:, g].reshape(2 * nc * md // cut, LANES) for g in range(cut)], j)
+            sx[n] = f.reshape(2 * nc, md // cut, LANES)
+            for i in range(2 * nc):
+                cross_copy(n, i).start()
+        keep(k, project(z, 1, jnp.concatenate([packed(got, g) for g in range(cut)], axis=0)))
+
+    head = pl.ds(0, LANES)
+    loaded(pv.at[0, head], 0)
+    send_p[0] = dot_nt(w_ref[...], pv[0, head])
+
     @pl.when(inner)
     def _():
-        for k in range(tblocks):
-            si[k] = project(mate, 1, mine[k, 0:panels]).reshape(nc, md, LANES)
-            for i in range(nc):
-                mate_copy(k, i).start()
+        pl.semaphore_wait(barrier, 3 + ntm - 1)
+
+    @pl.when(jnp.logical_not(inner))
+    def _():
+        pl.semaphore_wait(barrier, 2 + ntm - 1)
+
+    pair_copy(0).start()
+    rest = pl.ds(LANES, LANES)
+    loaded(pv.at[0, rest], 1)
+    mine[0] = dot_nt(w_ref[...], pv[0, rest])
+    merge(0)
+
+    @pl.when(inner)
+    def _():
+        pl.semaphore_signal(known, inc=1, device_id={"taps": far}, device_id_type=MESH)
+
+    prepare()
+
+    def aside(k):
+        si[k] = project(mate, 1, mine[k, 0:panels]).reshape(nc, md, LANES)
+        for j in range(nc):
+            mate_copy(k, j).start()
+
+    for k in range(1, tblocks):
+        sums(k)
+        pair_copy(k).start()
+        if k == 1:
+
+            @pl.when(inner)
+            def _():
+                aside(0)
+
+    @pl.when(inner)
+    def _():
+        for k in range(1, tblocks):
+            if k == tblocks - 1:
+                pl.semaphore_wait(known, 1)
+                pl.semaphore_signal(known, inc=1, device_id={"taps": mate}, device_id_type=MESH)
+                across(0)
+            merge(k)
+            aside(k)
+
+    @pl.when(jnp.logical_not(inner))
+    def _():
+        for k in range(1, tblocks):
+            merge(k)
 
     @pl.when(jnp.logical_not(inner))
     def _():
@@ -608,15 +670,8 @@
 
     @pl.when(inner)
     def _():
-        pl.semaphore_wait(known, 1)
-        pl.semaphore_signal(known, inc=1, device_id={"taps": mate}, device_id_type=MESH)
-        for k in range(tblocks):
-            up_copy(k).wait_recv()
-            total = mine[k, 0:panels] + up[k]
-            sx[k] = project(2 * (1 - side), 2, total).reshape(2 * nc, md, LANES)
-            for i in range(2 * nc):
-                cross_copy(k, i).start()
-            keep(k, project(z, 1, total))
+        for k in range(1, tblocks):
+            across(k)
 
     @pl.when(jnp.logical_not(inner))
     def _():
@@ -673,9 +728,12 @@
             for h in range(nc):
                 fb[h * tblocks + k] = fb[h * tblocks + k] + fi[k, h]
 
-        pltpu.make_async_copy(fx.at[k], fx.at[k], x_r.at[k]).wait()
+        for n in range(k * cut, (k + 1) * cut):
+            pltpu.make_async_copy(fx.at[n], fx.at[n], x_r.at[n]).wait()
         for h in range(nc):
-            fb[h * tblocks + k] = fb[h * tblocks + k] + fx[k, h]
+            parts = [fx[k * cut + j, h] for j in range(cut)]
+            come = jnp.concatenate([packed(parts, g) for g in range(cut)], axis=0)
+            fb[h * tblocks + k] = fb[h * tblocks + k] + come
         prefix([h * tblocks + k for h in range(nc)])
 
     re, im = jnp.zeros((md, LANES), f32), jnp.zeros((md, LANES), f32)
@@ -859,17 +917,18 @@
         pltpu.VMEM((md, LANES), f32),
         pltpu.VMEM((max(ntm - 1, 1), md, LANES), f32),
     ]
-    if nz == 4 and nc == 2 and tb % 2 == 0:
+    if nz == 4 and nc == 2:
         block = pltpu.VMEM((tb, rows, LANES), f32)
-        pieces = ((0, 1), (1, 1)) + tuple((b, 2) for b in range(2, tb, 2))
-        body = functools.partial(two_stage, (nz, nc, ntm, pieces))
+        body = functools.partial(two_stage, (nz, nc, ntm, CUT))
         scratch = (
-            inputs
+            inputs[:-2]
+            + [pltpu.VMEM((tb, nc * LANES, taps), jnp.bfloat16), inputs[-1]]
             + [pltpu.VMEM((modes, panels), jnp.bfloat16), block, block, block]
             + [
-                pltpu.VMEM((tb, panels, LANES), f32),
-                pltpu.VMEM((tb, 2 * nc, md, LANES), f32),
-                pltpu.VMEM((tb, nc, md, LANES), f32),
+                pltpu.VMEM((tb * CUT, panels // CUT, LANES), f32),
+                pltpu.VMEM((tb * CUT, panels // CUT, LANES), f32),
+                pltpu.VMEM((tb * CUT, 2 * nc, md // CUT, LANES), f32),
+                pltpu.VMEM((tb * CUT, nc, md // CUT, LANES), f32),
                 pltpu.VMEM((tb, nc, md, LANES), f32),
                 pltpu.VMEM((tb, nc, md, LANES), f32),
                 pltpu.VMEM((tb, md, LANES), f32),
@@ -885,8 +944,9 @@
                 pltpu.VMEM((owners - 1, fd, time_dev), f32),
                 pltpu.VMEM((max(ntm - 1, 1), owners, fd, time_dev), f32),
                 pltpu.VMEM((max(ntm - 1, 1), owners, fd, time_dev), f32),
-                dma((8,)), dma((2 * len(pieces),)),
-                dma(()), dma((tb,)), dma(()), dma((tb,)), dma(()), dma((tb,)), dma(()), dma((tb,)),
+                dma((8,)), dma((tb + 1,)),
+                dma(()), dma((tb,)), dma(()), dma((tb * CUT,)), dma(()), dma((tb * CUT,)),
+                dma(()), dma((tb,)),
                 dma(()), dma((tb,)), dma(()), dma(()), dma((ntm,)), dma((ntm,)), dma(()), dma(()),
                 dma((ntm,)), dma((ntm,)),
                 pltpu.SemaphoreType.REGULAR,

time: 30.9 us -> 29.3 us (0.948)
  Pallas kernels: 30.1 us -> 28.4 us
    pallas_call x1, Pallas kernels: 29.4 us -> 27.7 us  [on_device(): pl.pallas_call(body, out_shape=(pltpu.VMEM((md, time_dev), f32), pltpu.VM...]
where the time goes in v4:
time: 29.3 us; the launch traced here: 29.1 us
  Pallas kernels  28.4 us (97%)
  between operations  0.64 us (2%)
    pallas_call x1, Pallas kernels, on_device(): pl.pallas_call(body, out_shape=(pltpu.VMEM((md, time_dev), f32), pltpu.VM...  27.7 us
    pallas_call x1, Pallas kernels, on_device(): pl.pallas_call(write_out, out_shape=tuple((jax.ShapeDtypeStruct(o.shape,...  0.74 us

profile of v4, /device:TPU:0, one launch (start us, length us, event | category | flops | bytes accessed | tf_op | source)
XLA Modules:
  0.0 29.1 jit_solution(16598719060413688866)
XLA Ops:
  0.6 27.7 %shard_map.112 = (f32[64,1024]{1,0:T(8,128)S(1)}, f32[2,1024]{1,0:T(2,128)S(1)}, f32[2,1024]{1,0:T(2,128)S(1)}) custom-call(bf16[1024,2048]{1,0:T(8,128)(2,1)} %p_hbm.1, bf16[16,128]{1,0:T(8,128)(2,1)} %bitcast.8, s32[1,2048]{1,0:T(1,128)} %bitcast.6, s32[1,2048]{1,0:T(1,128)} %bitcast.7, bf16[256,512]{1,0:T(8,128)(2,1)} %shape_h.1, ...), custom_call_target="tpu_custom_call" | custom-call | tf_op jit(solution)/shard_map/pallas_call | solution.py:974
  28.3 0.7 %shard_map.113 = (f32[64,1024]{1,0:T(8,128)}, f32[2,1024]{1,0:T(2,128)}, f32[2,1024]{1,0:T(2,128)}) custom-call(f32[64,1024]{1,0:T(8,128)S(1)} %get-tuple-element.6.y, f32[2,1024]{1,0:T(2,128)S(1)} %get-tuple-element.7.fm, f32[2,1024]{1,0:T(2,128)S(1)} %get-tuple-element.8.fl), custom_call_target="tpu_custom_call" | custom-call | tf_op jit(solution)/shard_map/pallas_call | solution.py:1003

commit v5 on v4

--- a/solution.py
+++ b/solution.py
@@ -10,7 +10,7 @@
 MESH = pl.DeviceIdType.MESH
 LANES = 128
 LAG = 2
-CUT = 2
+CUT = 4
 VMEM_LIMIT = 32 * 1024 * 1024
 NT = (((1,), (1,)), ((), ()))
 
@@ -389,9 +389,10 @@
     area_ref, panel_ref, floor_ref, shape_ref, fshape_ref, order_ref, decay_ref, freq_ref, order_col,
     pv, w_ref, g_ref, send_p, recv_p, mine, mp, up, sx, fx, si, fi, sp, fb, tabs, loc, loc_im, ends, st_send, st_recv,
     fls, flr, fs, fr, cs, cr,
-    in_sem, p_sem, pp_s, pp_r, u_s, u_r, x_s, x_r, i_s, i_r, e_s, e_r, fl_s, fl_r, t_s, t_r, f_s, f_r, c_s, c_r, known,
+    in_sem, p_sem, pp_r, u_r, x_r, i_r, e_r, fl_r, t_s, t_r, f_r, c_s, c_r, known,
 ):
     nz, nc, ntm, cut = cfg
+    pp_s, u_s, i_s, x_s, e_s, fl_s, f_s = (in_sem.at[i] for i in range(7))
     owners = nz * nc
     z = lax.axis_index("taps")
     c = lax.axis_index("floors")
@@ -455,12 +456,6 @@
     ids = lax.broadcasted_iota(jnp.int32, (panels, LANES), 0)
     fids = lax.broadcasted_iota(jnp.int32, (floors, LANES), 0)
     area = area_ref[...].astype(f32)
-    for r in range(taps // LANES):
-        cols = slice(r * LANES, (r + 1) * LANES)
-        row = area[r : r + 1, :]
-        w_ref[0:panels, cols] = jnp.where(panel_ref[:, cols] == ids, row, 0.0).astype(bf16)
-        w_ref[panels:rows, cols] = jnp.where(floor_ref[:, cols] == fids, row, 0.0).astype(bf16)
-
     def sums(k):
         loaded(pv.at[k], k + 1)
         q = dot_nt(w_ref[...], pv[k])
@@ -530,14 +525,16 @@
 
     def mate_copy(k, i):
         return pltpu.make_async_remote_copy(
-            src_ref=si.at[k, i], dst_ref=fi.at[k, c], send_sem=i_s, recv_sem=i_r.at[k],
+            src_ref=si.at[k, i], dst_ref=fi.at[k, c], send_sem=i_s, recv_sem=i_r,
             device_id={"taps": mate, "floors": i}, device_id_type=MESH,
         )
 
     def cross_copy(k, i):
-        return pltpu.make_async_remote_copy(
-            src_ref=sx.at[k, i], dst_ref=fx.at[k, c], send_sem=x_s, recv_sem=x_r.at[k],
-            device_id={"taps": 2 * (1 - side) + i // nc, "floors": i % nc}, device_id_type=MESH,
+        chip = lax.rem(i // nc + 1 - side, 2)
+        return pltpu.make_async_remote_copy(
+            src_ref=sx.at[k, chip * nc + i % nc], dst_ref=fx.at[k // cut, k % cut, c],
+            send_sem=x_s, recv_sem=x_r.at[k // cut],
+            device_id={"taps": 2 * (1 - side) + chip, "floors": i % nc}, device_id_type=MESH,
         )
 
     def exchange(k):
@@ -569,7 +566,17 @@
 
     head = pl.ds(0, LANES)
     loaded(pv.at[0, head], 0)
-    send_p[0] = dot_nt(w_ref[...], pv[0, head])
+    chunk = 4 * LANES
+    first = jnp.zeros((rows, LANES), f32)
+    for start in range(0, taps, chunk):
+        for r in range(start // LANES, (start + chunk) // LANES):
+            cols = slice(r * LANES, (r + 1) * LANES)
+            row = area[r : r + 1, :]
+            w_ref[0:panels, cols] = jnp.where(panel_ref[:, cols] == ids, row, 0.0).astype(bf16)
+            w_ref[panels:rows, cols] = jnp.where(floor_ref[:, cols] == fids, row, 0.0).astype(bf16)
+        cols = slice(start, start + chunk)
+        first = first + dot_nt(w_ref[:, cols], pv[0, head, cols])
+    send_p[0] = first
 
     @pl.when(inner)
     def _():
@@ -614,6 +621,7 @@
                 across(0)
             merge(k)
             aside(k)
+        across(1)
 
     @pl.when(jnp.logical_not(inner))
     def _():
@@ -670,7 +678,7 @@
 
     @pl.when(inner)
     def _():
-        for k in range(1, tblocks):
+        for k in range(2, tblocks):
             across(k)
 
     @pl.when(jnp.logical_not(inner))
@@ -687,8 +695,6 @@
     def load_start(k, carry):
         load_copy(k).start()
         return carry
-
-    lax.fori_loop(1, owners, load_start, 0)
 
     def prefix(blks):
         parts = [fb[blk] * tabs[2 + i] for blk in blks for i in range(2)]
@@ -719,22 +725,26 @@
             device_id={"tm": to, "taps": j // nc, "floors": j % nc}, device_id_type=MESH,
         )
 
+    @pl.when(jnp.logical_not(inner))
+    def _():
+        pltpu.make_async_copy(fi, fi, i_r).wait()
+
     for k in range(tblocks):
         exchange(k).wait_recv()
 
         @pl.when(jnp.logical_not(inner))
         def _():
-            pltpu.make_async_copy(fi.at[k], fi.at[k], i_r.at[k]).wait()
             for h in range(nc):
                 fb[h * tblocks + k] = fb[h * tblocks + k] + fi[k, h]
 
-        for n in range(k * cut, (k + 1) * cut):
-            pltpu.make_async_copy(fx.at[n], fx.at[n], x_r.at[n]).wait()
+        pltpu.make_async_copy(fx.at[k], fx.at[k], x_r.at[k]).wait()
         for h in range(nc):
-            parts = [fx[k * cut + j, h] for j in range(cut)]
+            parts = [fx[k, j, h] for j in range(cut)]
             come = jnp.concatenate([packed(parts, g) for g in range(cut)], axis=0)
             fb[h * tblocks + k] = fb[h * tblocks + k] + come
         prefix([h * tblocks + k for h in range(nc)])
+        if k == tblocks - 2:
+            lax.fori_loop(1, owners, load_start, 0)
 
     re, im = jnp.zeros((md, LANES), f32), jnp.zeros((md, LANES), f32)
     ys = []
@@ -917,7 +927,7 @@
         pltpu.VMEM((md, LANES), f32),
         pltpu.VMEM((max(ntm - 1, 1), md, LANES), f32),
     ]
-    if nz == 4 and nc == 2:
+    if nz == 4 and nc == 2 and tb > 2:
         block = pltpu.VMEM((tb, rows, LANES), f32)
         body = functools.partial(two_stage, (nz, nc, ntm, CUT))
         scratch = (
@@ -928,7 +938,7 @@
                 pltpu.VMEM((tb * CUT, panels // CUT, LANES), f32),
                 pltpu.VMEM((tb * CUT, panels // CUT, LANES), f32),
                 pltpu.VMEM((tb * CUT, 2 * nc, md // CUT, LANES), f32),
-                pltpu.VMEM((tb * CUT, nc, md // CUT, LANES), f32),
+                pltpu.VMEM((tb, CUT, nc, md // CUT, LANES), f32),
                 pltpu.VMEM((tb, nc, md, LANES), f32),
                 pltpu.VMEM((tb, nc, md, LANES), f32),
                 pltpu.VMEM((tb, md, LANES), f32),
@@ -944,10 +954,8 @@
                 pltpu.VMEM((owners - 1, fd, time_dev), f32),
                 pltpu.VMEM((max(ntm - 1, 1), owners, fd, time_dev), f32),
                 pltpu.VMEM((max(ntm - 1, 1), owners, fd, time_dev), f32),
-                dma((8,)), dma((tb + 1,)),
-                dma(()), dma((tb,)), dma(()), dma((tb * CUT,)), dma(()), dma((tb * CUT,)),
-                dma(()), dma((tb,)),
-                dma(()), dma((tb,)), dma(()), dma(()), dma((ntm,)), dma((ntm,)), dma(()), dma(()),
+                dma((8,)), dma((tb + 1,)), dma((tb,)), dma((tb * CUT,)), dma((tb,)),
+                dma(()), dma((tb,)), dma(()), dma((ntm,)), dma((ntm,)), dma(()),
                 dma((ntm,)), dma((ntm,)),
                 pltpu.SemaphoreType.REGULAR,
             ]

time: 29.3 us -> 28.4 us (0.969)
  Pallas kernels: 28.4 us -> 27.6 us
    pallas_call x1, Pallas kernels: 27.7 us -> 26.9 us  [on_device(): pl.pallas_call(body, out_shape=(pltpu.VMEM((md, time_dev), f32), pltpu.VM...]
where the time goes in v5:
time: 28.4 us; the launch traced here: 28.3 us
  Pallas kernels  27.6 us (97%)
  between operations  0.64 us (2%)
    pallas_call x1, Pallas kernels, on_device(): pl.pallas_call(body, out_shape=(pltpu.VMEM((md, time_dev), f32), pltpu.VM...  26.9 us
    pallas_call x1, Pallas kernels, on_device(): pl.pallas_call(write_out, out_shape=tuple((jax.ShapeDtypeStruct(o.shape,...  0.74 us

profile of v5, /device:TPU:0, one launch (start us, length us, event | category | flops | bytes accessed | tf_op | source)
XLA Modules:
  0.0 28.3 jit_solution(18442032303134645667)
XLA Ops:
  0.6 26.9 %shard_map.112 = (f32[64,1024]{1,0:T(8,128)S(1)}, f32[2,1024]{1,0:T(2,128)S(1)}, f32[2,1024]{1,0:T(2,128)S(1)}) custom-call(bf16[1024,2048]{1,0:T(8,128)(2,1)} %p_hbm.1, bf16[16,128]{1,0:T(8,128)(2,1)} %bitcast.8, s32[1,2048]{1,0:T(1,128)} %bitcast.6, s32[1,2048]{1,0:T(1,128)} %bitcast.7, bf16[256,512]{1,0:T(8,128)(2,1)} %shape_h.1, ...), custom_call_target="tpu_custom_call" | custom-call | tf_op jit(solution)/shard_map/pallas_call | solution.py:982
  27.5 0.7 %shard_map.113 = (f32[64,1024]{1,0:T(8,128)}, f32[2,1024]{1,0:T(2,128)}, f32[2,1024]{1,0:T(2,128)}) custom-call(f32[64,1024]{1,0:T(8,128)S(1)} %get-tuple-element.6.y, f32[2,1024]{1,0:T(2,128)S(1)} %get-tuple-element.7.fm, f32[2,1024]{1,0:T(2,128)S(1)} %get-tuple-element.8.fl), custom_call_target="tpu_custom_call" | custom-call | tf_op jit(solution)/shard_map/pallas_call | solution.py:1011

commit v6 on v5

--- a/solution.py
+++ b/solution.py
@@ -24,6 +24,19 @@
     lo = (b - hi.astype(jnp.float32)).astype(jnp.bfloat16)
     return jnp.dot(a, hi, preferred_element_type=jnp.float32) + jnp.dot(
         a, lo, preferred_element_type=jnp.float32
+    )
+
+
+def hi_lo(b):
+    hi = b.astype(jnp.bfloat16)
+    return hi, (b - hi.astype(jnp.float32)).astype(jnp.bfloat16)
+
+
+def dot_stacked(a, b):
+    return jnp.dot(
+        jnp.concatenate([a, a], axis=1),
+        jnp.concatenate(hi_lo(b), axis=0),
+        preferred_element_type=jnp.float32,
     )
 
 
@@ -692,17 +705,13 @@
             device_id={"taps": j // nc, "floors": lax.rem(j, nc)}, device_id_type=MESH,
         )
 
-    def load_start(k, carry):
-        load_copy(k).start()
-        return carry
-
     def prefix(blks):
         parts = [fb[blk] * tabs[2 + i] for blk in blks for i in range(2)]
         v = jnp.concatenate(parts, axis=0)
-        hi = v.astype(bf16)
-        lo = (v - hi.astype(f32)).astype(bf16)
-        v = jnp.dot(hi, upto, preferred_element_type=f32) + jnp.dot(
-            lo, upto, preferred_element_type=f32
+        v = jnp.dot(
+            jnp.concatenate(hi_lo(v), axis=1),
+            jnp.concatenate([upto, upto], axis=0),
+            preferred_element_type=f32,
         )
         for n, blk in enumerate(blks):
             for i, dst in enumerate((loc, loc_im)):
@@ -713,15 +722,28 @@
     def response(blk, re, im):
         return tabs[0] * (loc[blk] + re) - tabs[1] * (loc_im[blk] + im)
 
+    def respond(start, stop, re, im):
+        ys = []
+        for blk in range(start, stop):
+            ys.append(response(blk, re, im))
+            re, im = turn(ends[blk, 0] + re, ends[blk, 1] + im)
+        y = jnp.concatenate(ys, axis=1)
+        cols = slice(start * LANES, stop * LANES)
+        part = dot_stacked(ls, y)
+        for j in range(owners):
+            fs[j, :, cols] = part[j * fd : (j + 1) * fd]
+        y_ref[:, cols] = y
+        return re, im
+
     def state_copy(to, src):
         return pltpu.make_async_remote_copy(
-            src_ref=st_send, dst_ref=st_recv.at[src], send_sem=t_s.at[to], recv_sem=t_r.at[src],
+            src_ref=st_send, dst_ref=st_recv.at[src], send_sem=t_s.at[to - 1], recv_sem=t_r.at[src],
             device_id={"tm": to}, device_id_type=MESH,
         )
 
     def carry_copy(to, src, j):
         return pltpu.make_async_remote_copy(
-            src_ref=cs.at[to - 1, j], dst_ref=cr.at[src, me], send_sem=c_s.at[to], recv_sem=c_r.at[src],
+            src_ref=cs.at[to - 1, j], dst_ref=cr.at[src, me], send_sem=c_s.at[to - 1], recv_sem=c_r.at[src],
             device_id={"tm": to, "taps": j // nc, "floors": j % nc}, device_id_type=MESH,
         )
 
@@ -744,18 +766,11 @@
             fb[h * tblocks + k] = fb[h * tblocks + k] + come
         prefix([h * tblocks + k for h in range(nc)])
         if k == tblocks - 2:
-            lax.fori_loop(1, owners, load_start, 0)
-
-    re, im = jnp.zeros((md, LANES), f32), jnp.zeros((md, LANES), f32)
-    ys = []
-    for blk in range(nb):
-        ys.append(response(blk, re, im))
-        re, im = turn(ends[blk, 0] + re, ends[blk, 1] + im)
-    y = jnp.concatenate(ys, axis=1)
-    y_ref[...] = y
-    part = dot_split(ls, y)
-    for j in range(owners):
-        fs[j] = part[j * fd : (j + 1) * fd]
+            for i in range(1, owners):
+                load_copy(i).start()
+            re, im = respond(0, k + 1, jnp.zeros((md, LANES), f32), jnp.zeros((md, LANES), f32))
+
+    re, im = respond(tblocks - 1, nb, re, im)
 
     def motion_copy(k):
         j = lax.rem(me + k, owners)
@@ -764,11 +779,8 @@
             device_id={"taps": j // nc, "floors": lax.rem(j, nc)}, device_id_type=MESH,
         )
 
-    def motion_start(k, carry):
+    for k in range(1, owners):
         motion_copy(k).start()
-        return carry
-
-    lax.fori_loop(1, owners, motion_start, 0)
     s_re, s_im = re, im
     for to in range(1, ntm):
 
@@ -784,7 +796,7 @@
             for blk in range(nb):
                 ys.append(tabs[0] * re - tabs[1] * im)
                 re, im = turn(re, im)
-            part = dot_split(ls, jnp.concatenate(ys, axis=1))
+            part = dot_stacked(ls, jnp.concatenate(ys, axis=1))
             for j in range(owners):
                 cs[to - 1, j] = part[j * fd : (j + 1) * fd]
             for j in range(owners):
@@ -875,7 +887,7 @@
 
         @pl.when(x < to)
         def _():
-            drain(cs.at[to - 1], c_s.at[to])
+            drain(cs.at[to - 1], c_s.at[to - 1])
 
 
 def write_out(y, fm, fl, y_out, fm_out, fl_out, sem):
@@ -929,6 +941,7 @@
     ]
     if nz == 4 and nc == 2 and tb > 2:
         block = pltpu.VMEM((tb, rows, LANES), f32)
+        later = dma((max(ntm - 1, 1),))
         body = functools.partial(two_stage, (nz, nc, ntm, CUT))
         scratch = (
             inputs[:-2]
@@ -955,8 +968,7 @@
                 pltpu.VMEM((max(ntm - 1, 1), owners, fd, time_dev), f32),
                 pltpu.VMEM((max(ntm - 1, 1), owners, fd, time_dev), f32),
                 dma((8,)), dma((tb + 1,)), dma((tb,)), dma((tb * CUT,)), dma((tb,)),
-                dma(()), dma((tb,)), dma(()), dma((ntm,)), dma((ntm,)), dma(()),
-                dma((ntm,)), dma((ntm,)),
+                dma(()), dma((tb,)), dma(()), later, later, dma(()), later, later,
                 pltpu.SemaphoreType.REGULAR,
             ]
         )

time: 28.4 us -> 28.4 us (level)
  no operation moved by 1% of the time
where the time goes in v6:
time: 28.4 us; the launch traced here: 28.2 us
  Pallas kernels  27.6 us (97%)
  between operations  0.64 us (2%)
    pallas_call x1, Pallas kernels, on_device(): pl.pallas_call(body, out_shape=(pltpu.VMEM((md, time_dev), f32), pltpu.VM...  26.8 us
    pallas_call x1, Pallas kernels, on_device(): pl.pallas_call(write_out, out_shape=tuple((jax.ShapeDtypeStruct(o.shape,...  0.74 us

profile of v6, /device:TPU:0, one launch (start us, length us, event | category | flops | bytes accessed | tf_op | source)
XLA Modules:
  0.0 28.2 jit_solution(17684778802083218103)
XLA Ops:
  0.6 26.8 %shard_map.112 = (f32[64,1024]{1,0:T(8,128)S(1)}, f32[2,1024]{1,0:T(2,128)S(1)}, f32[2,1024]{1,0:T(2,128)S(1)}) custom-call(bf16[1024,2048]{1,0:T(8,128)(2,1)} %p_hbm.1, bf16[16,128]{1,0:T(8,128)(2,1)} %bitcast.8, s32[1,2048]{1,0:T(1,128)} %bitcast.6, s32[1,2048]{1,0:T(1,128)} %bitcast.7, bf16[256,512]{1,0:T(8,128)(2,1)} %shape_h.1, ...), custom_call_target="tpu_custom_call" | custom-call | tf_op jit(solution)/shard_map/pallas_call | solution.py:994
  27.5 0.7 %shard_map.113 = (f32[64,1024]{1,0:T(8,128)}, f32[2,1024]{1,0:T(2,128)}, f32[2,1024]{1,0:T(2,128)}) custom-call(f32[64,1024]{1,0:T(8,128)S(1)} %get-tuple-element.6.y, f32[2,1024]{1,0:T(2,128)S(1)} %get-tuple-element.7.fm, f32[2,1024]{1,0:T(2,128)S(1)} %get-tuple-element.8.fl), custom_call_target="tpu_custom_call" | custom-call | tf_op jit(solution)/shard_map/pallas_call | solution.py:1023

commit v7 on v6

--- a/solution.py
+++ b/solution.py
@@ -751,6 +751,14 @@
     def _():
         pltpu.make_async_copy(fi, fi, i_r).wait()
 
+    def motion_copy(k, start, stop):
+        j = lax.rem(me + k, owners)
+        cols = pl.ds(start * LANES, (stop - start) * LANES)
+        return pltpu.make_async_remote_copy(
+            src_ref=fs.at[j, :, cols], dst_ref=fr.at[k - 1, :, cols], send_sem=f_s, recv_sem=f_r,
+            device_id={"taps": j // nc, "floors": lax.rem(j, nc)}, device_id_type=MESH,
+        )
+
     for k in range(tblocks):
         exchange(k).wait_recv()
 
@@ -760,6 +768,9 @@
                 fb[h * tblocks + k] = fb[h * tblocks + k] + fi[k, h]
 
         pltpu.make_async_copy(fx.at[k], fx.at[k], x_r.at[k]).wait()
+        if k == tblocks - 1:
+            for i in range(1, owners):
+                motion_copy(i, 0, k).start()
         for h in range(nc):
             parts = [fx[k, j, h] for j in range(cut)]
             come = jnp.concatenate([packed(parts, g) for g in range(cut)], axis=0)
@@ -772,15 +783,8 @@
 
     re, im = respond(tblocks - 1, nb, re, im)
 
-    def motion_copy(k):
-        j = lax.rem(me + k, owners)
-        return pltpu.make_async_remote_copy(
-            src_ref=fs.at[j], dst_ref=fr.at[k - 1], send_sem=f_s, recv_sem=f_r,
-            device_id={"taps": j // nc, "floors": lax.rem(j, nc)}, device_id_type=MESH,
-        )
-
     for k in range(1, owners):
-        motion_copy(k).start()
+        motion_copy(k, tblocks - 1, nb).start()
     s_re, s_im = re, im
     for to in range(1, ntm):
 

time: 28.4 us -> 28.2 us (level)
  no operation moved by 1% of the time
where the time goes in v7:
time: 28.2 us; the launch traced here: 28.1 us
  Pallas kernels  27.4 us (97%)
  between operations  0.64 us (2%)
    pallas_call x1, Pallas kernels, on_device(): pl.pallas_call(body, out_shape=(pltpu.VMEM((md, time_dev), f32), pltpu.VM...  26.7 us
    pallas_call x1, Pallas kernels, on_device(): pl.pallas_call(write_out, out_shape=tuple((jax.ShapeDtypeStruct(o.shape,...  0.74 us

profile of v7, /device:TPU:0, one launch (start us, length us, event | category | flops | bytes accessed | tf_op | source)
XLA Modules:
  0.0 28.1 jit_solution(12492397661766075332)
XLA Ops:
  0.6 26.7 %shard_map.112 = (f32[64,1024]{1,0:T(8,128)S(1)}, f32[2,1024]{1,0:T(2,128)S(1)}, f32[2,1024]{1,0:T(2,128)S(1)}) custom-call(bf16[1024,2048]{1,0:T(8,128)(2,1)} %p_hbm.1, bf16[16,128]{1,0:T(8,128)(2,1)} %bitcast.8, s32[1,2048]{1,0:T(1,128)} %bitcast.6, s32[1,2048]{1,0:T(1,128)} %bitcast.7, bf16[256,512]{1,0:T(8,128)(2,1)} %shape_h.1, ...), custom_call_target="tpu_custom_call" | custom-call | tf_op jit(solution)/shard_map/pallas_call | solution.py:998
  27.3 0.7 %shard_map.113 = (f32[64,1024]{1,0:T(8,128)}, f32[2,1024]{1,0:T(2,128)}, f32[2,1024]{1,0:T(2,128)}) custom-call(f32[64,1024]{1,0:T(8,128)S(1)} %get-tuple-element.6.y, f32[2,1024]{1,0:T(2,128)S(1)} %get-tuple-element.7.fm, f32[2,1024]{1,0:T(2,128)S(1)} %get-tuple-element.8.fl), custom_call_target="tpu_custom_call" | custom-call | tf_op jit(solution)/shard_map/pallas_call | solution.py:1027
